TPU v7x, 256 devices: a whole 4x4x8 slice. The times are simulated.
256 devices in a mesh: obs: 4 (over x), bfly: 64 (over z, y, core).
Axes of the slice: x: 4, y: 4, z: 8, core: 2. Of those that a mesh axis runs over, the one named last changes fastest.
Arguments:
- obs_field: float32 [262144, 1024], P(('obs', 'bfly')), may hold values from -6 to 6
- observer_leaf_bases: float32 [512, 512, 256], P(('obs', 'bfly')), may hold values from -0.25 to 0.25
- transfer: float32 [4, 512, 256, 512], P(None, ('obs', 'bfly')), may hold values from -0.25 to 0.25
- src_basis: float32 [128, 512, 256], P('bfly'), may hold values from -0.375 to 0.375
- leaf_map: int32 [4, 64], replicated, may hold values from 0 to 3, as said below
- partner_perm: int32 [4, 256], replicated, may hold values from 0 to 255, each once within a row
Outputs:
- src_field: float32 [1024, 65536], P('obs', 'bfly')
Inputs may be any that keep to these rules, and one draw needn't show every extreme that they name: In every column b, leaf_map[o, b] = (o + r_b) mod 4 for one offset r_b of that column, so each column names every observer group once. `partner_perm`: each row is a permutation of the rank indices.
All inputs are finite; a program needn't handle non-finite values.
Results may differ from a plain program's by a relative error of at most 0.0001.
Values sent between devices are 32-bit elements; how exact they have to be, the bound alone decides.
No kernel may reach another device: no remote copies, remote signals or barrier semaphores. Data moves between devices by JAX's collectives and lax.ppermute only.
A program may use at most 64 MiB of HBM per device.

v0:
```python
import jax
import jax.numpy as jnp
from jax import lax
from jax.sharding import PartitionSpec as P


def swapped(block, axis, apart):
    count = lax.axis_size(axis)
    route = []
    for low in range(count):
        high = low | 1 << apart
        if high != low and high < count:
            route += [(low, high), (high, low)]
    return lax.ppermute(block, axis, route)


def body(obs_field, observer_leaf_bases, transfer, src_basis, leaf_map, partner_perm):
    highest_level = lax.Precision.HIGHEST
    node_count, leaf_rows, rank_size = observer_leaf_bases.shape
    col_count = obs_field.shape[1]
    level_count = transfer.shape[0]
    n_groups = lax.axis_size("obs")
    obs_index = lax.axis_index("obs")
    bfly_index = lax.axis_index("bfly")
    block_list = obs_field.reshape(node_count, leaf_rows, col_count)
    projected_field = jnp.einsum(
        "jlr,jlc->jrc",
        observer_leaf_bases,
        block_list,
        precision=highest_level,
        preferred_element_type=jnp.float32,
    )
    source = leaf_map[obs_index, bfly_index]
    block_rows = node_count * rank_size
    flattened = projected_field.reshape(block_rows, col_count)
    target = source * block_rows
    shards = lax.all_gather(flattened, "obs", axis=0, tiled=True)
    first_row = jnp.int32(0)
    row_count = shards.shape[0]
    offset = jnp.clip(target, 0, row_count - block_rows)
    sliced_rows = lax.dynamic_slice_in_dim(shards, offset, block_rows, 0)
    inside = jnp.logical_and(target >= first_row, target < first_row + row_count)
    gathered = jnp.where(inside, sliced_rows, jnp.zeros_like(flattened))
    carried = gathered.reshape(node_count, rank_size, col_count)
    rank_index_list = jnp.arange(rank_size, dtype=jnp.int32)
    for level_index in range(level_count):
        partner = swapped(carried, "bfly", level_index)
        perm_row = partner_perm[level_index]
        onehot = (perm_row[:, None] == rank_index_list[None, :]).astype(jnp.float32)
        level_mats = transfer[level_index]
        own_part = level_mats[:, :, :rank_size]
        far_part = jnp.einsum(
            "jri,im->jrm",
            level_mats[:, :, rank_size:],
            onehot,
            precision=highest_level,
            preferred_element_type=jnp.float32,
        )
        own_term = jnp.einsum(
            "jrs,jsc->jrc",
            own_part,
            carried,
            precision=highest_level,
            preferred_element_type=jnp.float32,
        )
        far_term = jnp.einsum(
            "jrs,jsc->jrc",
            far_part,
            partner,
            precision=highest_level,
            preferred_element_type=jnp.float32,
        )
        carried = own_term + far_term
    share_cols = col_count // n_groups
    product = jnp.einsum(
        "jlr,jrc->cjl",
        src_basis,
        carried,
        precision=highest_level,
        preferred_element_type=jnp.float32,
    )
    return lax.psum_scatter(
        product.reshape(share_cols * lax.axis_size("obs"), node_count * leaf_rows),
        "obs",
        scatter_dimension=0,
        tiled=True,
    )


def solution(mesh):
    placed = (
        P(("obs", "bfly"), None),
        P(("obs", "bfly"), None, None),
        P(None, ("obs", "bfly"), None, None),
        P("bfly", None, None),
        P(),
        P(),
    )
    return jax.shard_map(
        body, mesh=mesh, in_specs=placed, out_specs=P("obs", "bfly"), check_vma=False
    )
```

profile of v0, /device:TPU:64, one launch (start us, length us, event | category | flops | bytes accessed | tf_op | source)
XLA Modules:
  0.0 330.6 jit_solution(14697301958873001551)
XLA Ops:
  6.5 7.6 %fusion.30 = f32[2,256,1024]{2,1,0:T(8,128)} fusion(f32[2,512,256]{2,1,0:T(8,128)} %param.7, f32[2,512,1024]{2,1,0:T(8,128)} %bitcast.70), kind=kOutput, calls=%fused_computation.43 | convolution fusion | flops 3221225472 | bytes 7340032 | tf_op jit(solution)/shard_map/jlr,jlc->jrc/dot_general | solution.py:26
  14.1 0.0 all-gather.2.cloned.1.call-update
  14.1 0.0 reduce-scatter.2.cloned.1.call-start
  14.2 1.3 dynamic_slice.6
  16.1 86.1 %all-gather.2.cloned.1.call-done = f32[2048,1024]{1,0:T(8,128)} async-done(((f32[512,1024]{1,0:T(8,128)}), f32[2048,1024]{1,0:T(8,128)}) %all-gather.2.cloned.1.call-update) | async-done | bytes 8388624 | tf_op jit(solution)/shard_map/all_gather | solution.py:37
  102.2 2.0 dynamic-slice_select_fusion
  104.2 0.3 collective-permute-start
  104.5 0.5 copy-done.1
  105.0 0.5 slice_bitcast_fusion
  105.5 0.5 convolution_bitcast_fusion.2
  105.9 3.4 %fusion.12 = f32[2,1024,256]{2,1,0:T(8,128)S(1)} fusion(f32[2,256,1024]{2,1,0:T(8,128)S(1)} %bitcast.69, f32[2,256,512]{2,1,0:T(8,128)S(1)} %get-tuple-element.7), kind=kOutput, calls=%fused_computation.24 | convolution fusion | flops 1610612736 | bytes 4718592 | tf_op jit(solution)/shard_map/jrs,jsc->jrc/dot_general | solution.py:59
  109.4 3.5 %bitcast_add_fusion.4 = f32[2,256,1024]{1,2,0:T(8,128)S(1)} fusion(f32[2,1024,256]{2,1,0:T(8,128)S(1)} %fusion.12, f32[2,256,256]{2,1,0:T(8,128)S(1)} %convolution_bitcast_fusion.2, f32[2,256,1024]{2,1,0:T(8,128)S(1)} %collective-permute-done), kind=kOutput, calls=%fused_computation.4 | convolution fusion | flops 1611137024 | bytes 6815744 | tf_op jit(solution)/shard_map/jrs,jsc->jrc/dot_general | solution.py:66
  112.9 1.8 collective-permute-start.1
  114.7 0.5 convolution_bitcast_fusion.1
  115.2 1.9 fusion.9
  117.1 43.6 %collective-permute-done.1 = f32[2,256,1024]{1,2,0:T(8,128)S(1)} collective-permute-done((f32[2,256,1024]{1,2,0:T(8,128)S(1)}, f32[2,256,1024]{1,2,0:T(8,128)S(1)}, u32[]{:S(2)}, u32[]{:S(2)}) %collective-permute-start.1) | collective-permute-done | bytes 2097184 | tf_op jit(solution)/shard_map/ppermute | solution.py:14
  160.8 2.1 bitcast_add_fusion.3
  162.9 3.1 collective-permute-start.2
  166.0 0.5 convolution_bitcast_fusion
  166.4 1.9 fusion.6
  168.4 42.8 %collective-permute-done.2 = f32[2,256,1024]{1,2,0:T(8,128)S(1)} collective-permute-done((f32[2,256,1024]{1,2,0:T(8,128)S(1)}, f32[2,256,1024]{1,2,0:T(8,128)S(1)}, u32[]{:S(2)}, u32[]{:S(2)}) %collective-permute-start.2) | collective-permute-done | bytes 2097184 | tf_op jit(solution)/shard_map/ppermute | solution.py:14
  211.1 2.0 bitcast_add_fusion.2
  213.2 1.9 collective-permute-start.3
  215.1 0.5 fusion.1
  215.6 0.4 copy.35
  216.0 2.0 fusion.3
  218.0 41.3 %collective-permute-done.3 = f32[2,256,1024]{1,2,0:T(8,128)S(1)} collective-permute-done((f32[2,256,1024]{1,2,0:T(8,128)S(1)}, f32[2,256,1024]{1,2,0:T(8,128)S(1)}, u32[]{:S(2)}, u32[]{:S(2)}) %collective-permute-start.3) | collective-permute-done | bytes 2097184 | tf_op jit(solution)/shard_map/ppermute | solution.py:14
  259.3 3.5 %fusion.14 = f32[2,256,1024]{2,1,0:T(8,128)S(1)} fusion(f32[2,256,1024]{1,2,0:T(8,128)S(1)} %collective-permute-done.3, f32[2,256,256]{1,0,2:T(2,128)S(1)} %bitcast.71), kind=kOutput, calls=%fused_computation.26 | convolution fusion | flops 1610612736 | bytes 4718592 | tf_op jit(solution)/shard_map/jrs,jsc->jrc/dot_general | solution.py:66
  262.8 5.1 %fusion = f32[2,1024,512]{1,2,0:T(8,128)} fusion(f32[2,512,256]{2,1,0:T(8,128)S(1)} %copy-done, f32[2,256,1024]{2,1,0:T(8,128)S(1)} %fusion.14, f32[2,1024,256]{1,2,0:T(8,128)S(1)} %fusion.3), kind=kOutput, calls=%fused_computation.1 | convolution fusion | flops 3221749760 | bytes 9437184 | tf_op jit(solution)/shard_map/jlr,jrc->cjl/dot_general | solution.py:75
  267.9 5.4 %copy.22 = f32[1024,1024]{1,0:T(8,128)} copy(f32[1024,1024]{0,1:T(8,128)} %bitcast.66) | data formatting | bytes 8388608 | tf_op jit(solution)/shard_map/reshape | solution.py:83
  273.3 0.0 reduce-scatter.2.cloned.1.call-update
  273.3 50.5 %reduce-scatter.2.cloned.1.call-done = f32[256,1024]{1,0:T(8,128)} async-done(((f32[1024,1024]{1,0:T(8,128)}), f32[256,1024]{1,0:T(8,128)}) %reduce-scatter.2.cloned.1.call-update) | async-done | bytes 1048592 | tf_op jit(solution)/shard_map/reduce_scatter | solution.py:82
  (8 shorter events, 0.0 us)
Async XLA Ops:
  6.5 256.2 %copy-start = (f32[2,512,256]{2,1,0:T(8,128)S(1)}, f32[2,512,256]{2,1,0:T(8,128)}, u32[]{:S(2)}) copy-start(f32[2,512,256]{2,1,0:T(8,128)} %param.9) | copy-start | bytes 3145732
  6.5 95.7 %all-gather.2.cloned.1.call-start = ((), (), s32[]{:S(2)}) async-start(), calls=%async_computation.1 | async-start | bytes 10485760 | tf_op jit(solution)/shard_map/all_gather | solution.py:37
  14.1 90.4 %copy-start.2 = (s32[4,256]{1,0:T(4,128)S(1)}, s32[4,256]{1,0:T(4,128)}, u32[]{:S(2)}) copy-start(s32[4,256]{1,0:T(4,128)} %param.11) | copy-start | bytes 12292
  14.1 309.7 %reduce-scatter.2.cloned.1.call-start = ((), (), s32[]{:S(2)}) async-start(), calls=%async_computation.2 | async-start | bytes 5242880 | tf_op jit(solution)/shard_map/reduce_scatter | solution.py:82
  102.2 2.8 copy-start.1
  104.2 5.2 %collective-permute-start = (f32[2,256,1024]{2,1,0:T(8,128)S(1)}, f32[2,256,1024]{2,1,0:T(8,128)S(1)}, u32[]{:S(2)}, u32[]{:S(2)}) collective-permute-start(f32[2,256,1024]{2,1,0:T(8,128)S(1)} %bitcast.68), channel_id=1, source_target_pairs={{0,1},{1,0},{2,3},{3,2},{4,5},{5,4},{6,7},{7,6},{8,9},{9,8},{10,11... | collective-permute-start | bytes 6291464 | tf_op jit(solution)/shard_map/ppermute | solution.py:14
  112.9 47.8 %collective-permute-start.1 = (f32[2,256,1024]{1,2,0:T(8,128)S(1)}, f32[2,256,1024]{1,2,0:T(8,128)S(1)}, u32[]{:S(2)}, u32[]{:S(2)}) collective-permute-start(f32[2,256,1024]{1,2,0:T(8,128)S(1)} %bitcast_add_fusion.4), channel_id=1, source_target_pairs={{0,2},{2,0},{1,3},{3,1},{4,6},{6,4},{5,7},{7,5},{8,10},{10,8},{9,1... | collective-permute-start | bytes 6291464 | tf_op jit(solution)/shard_map/ppermute | solution.py:14
  162.9 48.3 %collective-permute-start.2 = (f32[2,256,1024]{1,2,0:T(8,128)S(1)}, f32[2,256,1024]{1,2,0:T(8,128)S(1)}, u32[]{:S(2)}, u32[]{:S(2)}) collective-permute-start(f32[2,256,1024]{1,2,0:T(8,128)S(1)} %bitcast_add_fusion.3), channel_id=1, source_target_pairs={{0,4},{4,0},{1,5},{5,1},{2,6},{6,2},{3,7},{7,3},{8,12},{12,8},{9,1... | collective-permute-start | bytes 6291464 | tf_op jit(solution)/shard_map/ppermute | solution.py:14
  213.2 46.1 %collective-permute-start.3 = (f32[2,256,1024]{1,2,0:T(8,128)S(1)}, f32[2,256,1024]{1,2,0:T(8,128)S(1)}, u32[]{:S(2)}, u32[]{:S(2)}) collective-permute-start(f32[2,256,1024]{1,2,0:T(8,128)S(1)} %bitcast_add_fusion.2), channel_id=1, source_target_pairs={{0,8},{8,0},{1,9},{9,1},{2,10},{10,2},{3,11},{11,3},{4,12},{12,4},... | collective-permute-start | bytes 6291464 | tf_op jit(solution)/shard_map/ppermute | solution.py:14
Sparse Core Ops, SparseCore 0:
  14.2 87.8 all-gather.1
  273.4 50.3 reduce-scatter.1
where the time goes:
time: 332 us; the launch traced here: 331 us
  waiting for transfers between devices  264 us (80%)
  matrix products  35 us (11%)
  between operations  14.2 us (4%)
  local copies, waits for them, and re-layouts  8.02 us (2%)
  starting transfers between devices  7.11 us (2%)
    ppermute x4, waiting for transfers between devices, swapped(): return lax.ppermute(block, axis, route)  128 us
    all_gather x1, waiting for transfers between devices, body(): shards = lax.all_gather(flattened, 'obs', axis=0, tiled=True)  86.1 us
    reduce_scatter x1, waiting for transfers between devices, body(): lax.psum_scatter(product.reshape(share_cols * lax.axis_size('obs'), node_...  50.5 us
    dot_general x4, matrix products, body(): jnp.einsum('jrs,jsc->jrc', far_part, partner, precision=highest_level, pr...  11.1 us
    dot_general x4, matrix products, body(): jnp.einsum('jrs,jsc->jrc', own_part, carried, precision=highest_level, pr...  9.3 us
    dot_general x1, matrix products, body(): jnp.einsum('jlr,jlc->jrc', observer_leaf_bases, block_list, precision=hig...  7.56 us
    ppermute x4, starting transfers between devices, swapped(): return lax.ppermute(block, axis, route)  7.06 us
  transfers between devices with their start and end apart: 6, of which 5 were waited for; matrix products, arithmetic and copies ran while one was open for 4% of the time, Pallas kernels for 0%

commit v1 on v0

v1 whole, which is shorter than its diff:
```python
import functools

import jax
import jax.numpy as jnp
from jax import lax
from jax.experimental import pallas as pl
from jax.experimental.pallas import tpu as pltpu
from jax.sharding import PartitionSpec as P

CHUNKS = ((0, 0, 128), (0, 128, 128), (1, 0, 128), (1, 128, 128))
ORDER = (0, 1, 2, 3, 0, 1, 0, 2, 1, 0, 3, 2, 1, 0, 3, 2, 1, 0, 3, 2, 1, 0, 3, 2, 1, 0, 3, 2, 1, 0, 3, 2, 1, 3, 2, 3)
LIMIT = 12 << 20
CHEAP = pl.CostEstimate(flops=0, transcendentals=0, bytes_accessed=0)
NT = (((1,), (1,)), ((), ()))
TN = (((0,), (0,)), ((), ()))


def flipped(block, axis, mask):
    count = lax.axis_size(axis)
    return lax.ppermute(block, axis, [(i, i ^ mask) for i in range(count)])


def halves(block):
    high = block.astype(jnp.bfloat16)
    return high, (block - high.astype(jnp.float32)).astype(jnp.bfloat16)


def dot(a, b, dims):
    return lax.dot_general(a, b, dims, preferred_element_type=jnp.float32)


def dot3(a, b, dims):
    (ah, al), (bh, bl) = a, b
    return dot(ah, bh, dims) + (dot(ah, bl, dims) + dot(al, bh, dims))


def project_kernel(block, basis, out, high, low):
    @pl.when(pl.program_id(0) == 0)
    def _():
        high[...], low[...] = halves(basis[0])

    out[...] = dot3(halves(block[...]), (high[...], low[...]), TN)


def project(obs_field, bases, node, at, width):
    nodes, leaf, rank = bases.shape
    share = obs_field.shape[1] // 4
    return pl.pallas_call(
        project_kernel,
        grid=(4,),
        in_specs=[
            pl.BlockSpec(
                (leaf, width), lambda i: (node, (3 * i) % 4 * (share // width) + at // width)
            ),
            pl.BlockSpec((1, leaf, rank), lambda i: (node, 0, 0)),
        ],
        out_specs=pl.BlockSpec((width, rank), lambda i: (i, 0)),
        out_shape=jax.ShapeDtypeStruct((4 * width, rank), jnp.float32),
        scratch_shapes=[pltpu.VMEM((leaf, rank), jnp.bfloat16)] * 2,
        compiler_params=pltpu.CompilerParams(vmem_limit_bytes=LIMIT),
        cost_estimate=CHEAP,
    )(obs_field, bases)


def prepare_kernel(first, perm, mats, high, low):
    rank = mats.shape[2]
    h, l = halves(mats[0, 0])
    row = perm[pl.ds(first + pl.program_id(0), 1), :]
    picks = lax.broadcasted_iota(jnp.int32, (rank, rank), 0)
    onehot = (row == picks).astype(jnp.bfloat16)
    dims = NT
    for out, part in ((high, h), (low, l)):
        out[0, 0, :, :rank] = part[:, :rank]
        out[0, 0, :, rank:] = dot(part[:, rank:], onehot, dims).astype(jnp.bfloat16)


def prepare(mats, perm, first):
    levels, nodes, rank, two = mats.shape
    spec = pl.BlockSpec((1, 1, rank, two), lambda k, j: (k, j, 0, 0))
    return pl.pallas_call(
        functools.partial(prepare_kernel, first),
        grid=(levels, nodes),
        in_specs=[pl.BlockSpec(perm.shape, lambda k, j: (0, 0)), spec],
        out_specs=[spec, spec],
        out_shape=[jax.ShapeDtypeStruct(mats.shape, jnp.bfloat16)] * 2,
        compiler_params=pltpu.CompilerParams(vmem_limit_bytes=LIMIT),
        cost_estimate=CHEAP,
    )(perm, mats)


def step_kernel(a, b, high, low, out):
    rank = a.shape[1]
    h, l = high[0, 0], low[0, 0]
    out[...] = dot3(halves(a[...]), (h[:, :rank], l[:, :rank]), NT) + dot3(
        halves(b[...]), (h[:, rank:], l[:, rank:]), NT
    )


def step(a, b, mats, k, j):
    whole = pl.BlockSpec(a.shape, lambda i: (0, 0))
    one = pl.BlockSpec((1, 1) + mats[0].shape[2:], lambda i: (k, j, 0, 0))
    return pl.pallas_call(
        step_kernel,
        grid=(1,),
        in_specs=[whole, whole, one, one],
        out_specs=whole,
        out_shape=jax.ShapeDtypeStruct(a.shape, jnp.float32),
        compiler_params=pltpu.CompilerParams(vmem_limit_bytes=LIMIT),
        cost_estimate=CHEAP,
    )(a, b, *mats)


def body(obs_field, observer_leaf_bases, transfer, src_basis, leaf_map, partner_perm):
    nodes, leaf, rank = observer_leaf_bases.shape
    x = lax.axis_index("obs")
    b = lax.axis_index("bfly")

    wanted = leaf_map[x, b]
    wanted_there = leaf_map[x ^ 3, b]
    outer = jnp.where((x == 0) | (x == 3), 0, 1)
    inner = x & 1
    flags = (
        wanted_there == (x ^ 1), wanted == x, wanted == (x ^ 1),
        outer == 0, inner == 0,
    )
    flags, obs_field, transfer, partner_perm = lax.optimization_barrier(
        (flags, obs_field, transfer, partner_perm)
    )
    pass_on, stays, from_near, outer, inner = flags

    mats_there = flipped(transfer[1], "bfly", 2)
    mats = prepare(transfer, partner_perm, 0)
    there = prepare(mats_there[None], partner_perm, 1)

    def chain(n, bases):
        j, at, width = CHUNKS[n]
        own = project(obs_field, bases, j, at, width)
        near = yield own, flipped(own, "obs", 1)
        sent = jnp.where(pass_on, near, own)
        far = yield sent, flipped(sent, "obs", 3)
        c = jnp.where(stays, own, jnp.where(from_near, near, far))
        p = yield c, flipped(c, "bfly", 1)
        c = step(c, p, mats, 0, j)
        p = yield c, flipped(c, "bfly", 2)
        d = step(p, c, there, 0, j)
        q = yield d, flipped(d, "bfly", 6)
        c = step(c, p, mats, 1, j)
        c = step(c, q, mats, 2, j)
        p = yield c, flipped(c, "bfly", 8)
        c = step(c, p, mats, 3, j)
        top, end = c[: 2 * width], c[2 * width :]
        sent = jnp.where(outer, end, top)
        got = yield sent, flipped(sent, "obs", 1)
        c = jnp.where(outer, top, end) + got
        top, end = c[:width], c[width:]
        sent = jnp.where(inner, end, top)
        got = yield sent, flipped(sent, "obs", 3)
        c = jnp.where(inner, top, end) + got
        out = lax.dot_general(
            c, src_basis[j], NT, precision=lax.Precision.HIGHEST,
            preferred_element_type=jnp.float32,
        )
        yield out, out

    chains = {}
    waiting = {}
    last = None
    for n in ORDER:
        if n not in chains:
            bases = observer_leaf_bases
            if last is not None:
                bases, _ = lax.optimization_barrier((bases, last))
            chains[n] = chain(n, bases)
            last, waiting[n] = next(chains[n])
        else:
            value, _ = lax.optimization_barrier((waiting[n], last))
            last, waiting[n] = chains[n].send(value)
    rows = {}
    for n, (node, at, width) in enumerate(CHUNKS):
        rows.setdefault(node, {})[at] = waiting[n]
    return jnp.concatenate(
        [
            jnp.concatenate([rows[node][at] for at in sorted(rows[node])], 0)
            for node in range(nodes)
        ],
        1,
    )


def solution(mesh):
    placed = (
        P(("obs", "bfly"), None),
        P(("obs", "bfly"), None, None),
        P(None, ("obs", "bfly"), None, None),
        P("bfly", None, None),
        P(),
        P(),
    )
    return jax.shard_map(
        body, mesh=mesh, in_specs=placed, out_specs=P("obs", "bfly"), check_vma=False
    )
```

time: 332 us -> 143 us (0.43)
  waiting for transfers between devices: 264 us -> 58.6 us
  starting transfers between devices: 7.11 us -> 50.6 us
  matrix products: 35 us -> 2.53 us
  Pallas kernels: 0 us -> 21.8 us
  between operations: 14.2 us -> 2.41 us
    all_gather x1 -> x0, waiting for transfers between devices: 86.1 us -> none  [body(): shards = lax.all_gather(flattened, 'obs', axis=0, tiled=True)]
    ppermute x4 -> x33, waiting for transfers between devices: 128 us -> 58.6 us  [flipped(): return lax.ppermute(block, axis, [(i, i ^ mask) for i in range(count)])]
    reduce_scatter x1 -> x0, waiting for transfers between devices: 50.5 us -> none  [body(): lax.psum_scatter(product.reshape(share_cols * lax.axis_size('obs'), node_...]
    ppermute x4 -> x33, starting transfers between devices: 7.06 us -> 50.6 us  [flipped(): return lax.ppermute(block, axis, [(i, i ^ mask) for i in range(count)])]
    dot_general x14 -> x4, matrix products: 35 us -> 2.53 us  [chain(): lax.dot_general(c, src_basis[j], NT, precision=lax.Precision.HIGHEST, pre...]
    pallas_call x0 -> x26, Pallas kernels: none -> 21.8 us  [the longest x20 12.4 us: step(): pl.pallas_call(step_kernel, grid=(1,), in_specs=[whole, whole, one, one],...]
    reshape x1 -> x0, local copies, waits for them, and re-layouts: 5.38 us -> none  [body(): product.reshape(share_cols * lax.axis_size('obs'), node_count * leaf_rows)]
  transfers between devices with their start and end apart: 6 -> 33, of which waited for: 5 -> 18; matrix products, arithmetic and copies ran while one was open for 4% -> 2% of each run, Pallas kernels for 0% -> 14%
where the time goes in v1:
time: 143 us
  waiting for transfers between devices  58.6 us (41%)
  starting transfers between devices  50.6 us (35%)
  Pallas kernels  21.8 us (15%)
  local copies, waits for them, and re-layouts  4.89 us (3%)
  matrix products  2.53 us (2%)
  between operations  2.41 us (2%)
  other arithmetic  2.16 us (2%)
    ppermute x33, waiting for transfers between devices, flipped(): return lax.ppermute(block, axis, [(i, i ^ mask) for i in range(count)])  58.6 us
    ppermute x33, starting transfers between devices, flipped(): return lax.ppermute(block, axis, [(i, i ^ mask) for i in range(count)])  50.6 us
    pallas_call x20, Pallas kernels, step(): pl.pallas_call(step_kernel, grid=(1,), in_specs=[whole, whole, one, one],...  12.4 us
    pallas_call x4, Pallas kernels, project(): pl.pallas_call(project_kernel, grid=(4,), in_specs=[pl.BlockSpec((leaf, w...  6.4 us
    unnamed x10, local copies, waits for them, and re-layouts  3.43 us
    pallas_call x2, Pallas kernels, prepare(): pl.pallas_call(functools.partial(prepare_kernel, first), grid=(levels, no...  3.01 us
  transfers between devices with their start and end apart: 33, of which 18 were waited for; matrix products, arithmetic and copies ran while one was open for 2% of the time, Pallas kernels for 14%

profile of v1, /device:TPU:64, one launch (start us, length us, event | category | flops | bytes accessed | tf_op | source)
XLA Modules:
  0.0 143.0 jit_solution(316222545031893744)
XLA Ops:
  3.3 2.2 %copy-done = f32[1024,1024]{1,0:T(8,128)S(1)} copy-done((f32[1024,1024]{1,0:T(8,128)S(1)}, f32[1024,1024]{1,0:T(8,128)}, u32[]{:S(2)}) %copy-start) | copy-done | bytes 4194328
  17.6 5.7 %collective-permute-done = f32[512,256]{1,0:T(8,128)S(1)} collective-permute-done((f32[512,256]{1,0:T(8,128)S(1)}, f32[512,256]{1,0:T(8,128)S(1)}, u32[]{:S(2)}, u32[]{:S(2)}) %collective-permute-start) | collective-permute-done | bytes 524320 | tf_op jit(solution)/shard_map/ppermute | solution.py:20
  23.3 2.8 %collective-permute-start.1 = (f32[512,256]{1,0:T(8,128)S(1)}, f32[512,256]{1,0:T(8,128)S(1)}, u32[]{:S(2)}, u32[]{:S(2)}) collective-permute-start(f32[512,256]{1,0:T(8,128)S(1)} %broadcast_select_fusion.3), channel_id=1, source_target_pairs={{0,192},{64,128},{128,64},{192,0},{1,193},{65,129},{129,65},{193,1... | collective-permute-start | bytes 1572872 | tf_op jit(solution)/shard_map/ppermute | solution.py:20
  26.3 1.7 %collective-permute-start.10 = (f32[2,256,512]{2,1,0:T(8,128)S(1)}, f32[2,256,512]{2,1,0:T(8,128)S(1)}, u32[]{:S(2)}, u32[]{:S(2)}) collective-permute-start(f32[2,256,512]{2,1,0:T(8,128)S(1)} %slice_bitcast_fusion), channel_id=1, source_target_pairs={{0,2},{1,3},{2,0},{3,1},{4,6},{5,7},{6,4},{7,5},{8,10},{9,11},{10,... | collective-permute-start | bytes 3145736 | tf_op jit(solution)/shard_map/ppermute | solution.py:20
  27.9 2.4 %shard_map.68 = (bf16[4,2,256,512]{3,2,1,0:T(8,128)(2,1)S(1)}, bf16[4,2,256,512]{3,2,1,0:T(8,128)(2,1)S(1)}) custom-call(s32[4,256]{1,0:T(4,128)S(1)} %copy-done.3, f32[4,2,256,512]{3,2,1,0:T(8,128)S(1)} %copy-done.2), custom_call_target="tpu_custom_call" | custom-call | tf_op jit(solution)/shard_map/pallas_call | solution.py:80
  30.3 4.2 %collective-permute-done.2 = f32[512,256]{1,0:T(8,128)S(1)} collective-permute-done((f32[512,256]{1,0:T(8,128)S(1)}, f32[512,256]{1,0:T(8,128)S(1)}, u32[]{:S(2)}, u32[]{:S(2)}) %collective-permute-start.2) | collective-permute-done | bytes 524320 | tf_op jit(solution)/shard_map/ppermute | solution.py:20
  34.6 2.8 %collective-permute-start.4 = (f32[512,256]{1,0:T(8,128)S(1)}, f32[512,256]{1,0:T(8,128)S(1)}, u32[]{:S(2)}, u32[]{:S(2)}) collective-permute-start(f32[512,256]{1,0:T(8,128)S(1)} %broadcast_select_fusion.2), channel_id=1, source_target_pairs={{0,192},{64,128},{128,64},{192,0},{1,193},{65,129},{129,65},{193,1... | collective-permute-start | bytes 1572872 | tf_op jit(solution)/shard_map/ppermute | solution.py:20
  37.6 8.1 %collective-permute-done.5 = f32[512,256]{1,0:T(8,128)S(1)} collective-permute-done((f32[512,256]{1,0:T(8,128)S(1)}, f32[512,256]{1,0:T(8,128)S(1)}, u32[]{:S(2)}, u32[]{:S(2)}) %collective-permute-start.5) | collective-permute-done | bytes 524320 | tf_op jit(solution)/shard_map/ppermute | solution.py:20
  45.8 2.8 %collective-permute-start.8 = (f32[512,256]{1,0:T(8,128)S(1)}, f32[512,256]{1,0:T(8,128)S(1)}, u32[]{:S(2)}, u32[]{:S(2)}) collective-permute-start(f32[512,256]{1,0:T(8,128)S(1)} %broadcast_select_fusion.1), channel_id=1, source_target_pairs={{0,192},{64,128},{128,64},{192,0},{1,193},{65,129},{129,65},{193,1... | collective-permute-start | bytes 1572872 | tf_op jit(solution)/shard_map/ppermute | solution.py:20
  49.5 1.6 %collective-permute-start.6 = (f32[512,256]{1,0:T(8,128)S(1)}, f32[512,256]{1,0:T(8,128)S(1)}, u32[]{:S(2)}, u32[]{:S(2)}) collective-permute-start(f32[512,256]{1,0:T(8,128)S(1)} %shard_map.69.a.b), channel_id=1, source_target_pairs={{0,2},{1,3},{2,0},{3,1},{4,6},{5,7},{6,4},{7,5},{8,10},{9,11},{10,... | collective-permute-start | bytes 1572872 | tf_op jit(solution)/shard_map/ppermute | solution.py:20
  51.2 4.6 %collective-permute-done.9 = f32[512,256]{1,0:T(8,128)S(1)} collective-permute-done((f32[512,256]{1,0:T(8,128)S(1)}, f32[512,256]{1,0:T(8,128)S(1)}, u32[]{:S(2)}, u32[]{:S(2)}) %collective-permute-start.9) | collective-permute-done | bytes 524320 | tf_op jit(solution)/shard_map/ppermute | solution.py:20
  55.9 2.8 %collective-permute-start.14 = (f32[512,256]{1,0:T(8,128)S(1)}, f32[512,256]{1,0:T(8,128)S(1)}, u32[]{:S(2)}, u32[]{:S(2)}) collective-permute-start(f32[512,256]{1,0:T(8,128)S(1)} %broadcast_select_fusion), channel_id=1, source_target_pairs={{0,192},{64,128},{128,64},{192,0},{1,193},{65,129},{129,65},{193,1... | collective-permute-start | bytes 1572872 | tf_op jit(solution)/shard_map/ppermute | solution.py:20
  59.6 1.7 %collective-permute-start.12 = (f32[512,256]{1,0:T(8,128)S(1)}, f32[512,256]{1,0:T(8,128)S(1)}, u32[]{:S(2)}, u32[]{:S(2)}) collective-permute-start(f32[512,256]{1,0:T(8,128)S(1)} %shard_map.70.b.a), channel_id=1, source_target_pairs={{0,2},{1,3},{2,0},{3,1},{4,6},{5,7},{6,4},{7,5},{8,10},{9,11},{10,... | collective-permute-start | bytes 1572872 | tf_op jit(solution)/shard_map/ppermute | solution.py:20
  61.9 2.5 %collective-permute-done.6.b.a = f32[512,256]{1,0:T(8,128)S(1)} collective-permute-done((f32[512,256]{1,0:T(8,128)S(1)}, f32[512,256]{1,0:T(8,128)S(1)}, u32[]{:S(2)}, u32[]{:S(2)}) %collective-permute-start.6) | collective-permute-done | bytes 524320 | tf_op jit(solution)/shard_map/ppermute | solution.py:20
  64.9 3.3 %collective-permute-start.11 = (f32[512,256]{1,0:T(8,128)S(1)}, f32[512,256]{1,0:T(8,128)S(1)}, u32[]{:S(2)}, u32[]{:S(2)}) collective-permute-start(f32[512,256]{1,0:T(8,128)S(1)} %shard_map.73), channel_id=1, source_target_pairs={{0,6},{1,7},{2,4},{3,5},{4,2},{5,3},{6,0},{7,1},{8,14},{9,15},{10,... | collective-permute-start | bytes 1572872 | tf_op jit(solution)/shard_map/ppermute | solution.py:20
  68.2 1.8 %collective-permute-done.14 = f32[512,256]{1,0:T(8,128)S(1)} collective-permute-done((f32[512,256]{1,0:T(8,128)S(1)}, f32[512,256]{1,0:T(8,128)S(1)}, u32[]{:S(2)}, u32[]{:S(2)}) %collective-permute-start.14) | collective-permute-done | bytes 524320 | tf_op jit(solution)/shard_map/ppermute | solution.py:20
  70.8 1.7 %collective-permute-start.17 = (f32[512,256]{1,0:T(8,128)S(1)}, f32[512,256]{1,0:T(8,128)S(1)}, u32[]{:S(2)}, u32[]{:S(2)}) collective-permute-start(f32[512,256]{1,0:T(8,128)S(1)} %shard_map.74.b.a), channel_id=1, source_target_pairs={{0,2},{1,3},{2,0},{3,1},{4,6},{5,7},{6,4},{7,5},{8,10},{9,11},{10,... | collective-permute-start | bytes 1572872 | tf_op jit(solution)/shard_map/ppermute | solution.py:20
  72.5 3.1 %collective-permute-done.12.a.b = f32[512,256]{1,0:T(8,128)S(1)} collective-permute-done((f32[512,256]{1,0:T(8,128)S(1)}, f32[512,256]{1,0:T(8,128)S(1)}, u32[]{:S(2)}, u32[]{:S(2)}) %collective-permute-start.12) | collective-permute-done | bytes 524320 | tf_op jit(solution)/shard_map/ppermute | solution.py:20
  76.2 3.1 %collective-permute-start.16 = (f32[512,256]{1,0:T(8,128)S(1)}, f32[512,256]{1,0:T(8,128)S(1)}, u32[]{:S(2)}, u32[]{:S(2)}) collective-permute-start(f32[512,256]{1,0:T(8,128)S(1)} %shard_map.75), channel_id=1, source_target_pairs={{0,6},{1,7},{2,4},{3,5},{4,2},{5,3},{6,0},{7,1},{8,14},{9,15},{10,... | collective-permute-start | bytes 1572872 | tf_op jit(solution)/shard_map/ppermute | solution.py:20
  80.5 2.0 %collective-permute-start.15 = (f32[512,256]{1,0:T(8,128)S(1)}, f32[512,256]{1,0:T(8,128)S(1)}, u32[]{:S(2)}, u32[]{:S(2)}) collective-permute-start(f32[512,256]{1,0:T(8,128)S(1)} %shard_map.76.a), channel_id=1, source_target_pairs={{0,8},{1,9},{2,10},{3,11},{4,12},{5,13},{6,14},{7,15},{8,0},{9,1},... | collective-permute-start | bytes 1572872 | tf_op jit(solution)/shard_map/ppermute | solution.py:20
  84.0 2.8 %collective-permute-done.17.a.b = f32[512,256]{1,0:T(8,128)S(1)} collective-permute-done((f32[512,256]{1,0:T(8,128)S(1)}, f32[512,256]{1,0:T(8,128)S(1)}, u32[]{:S(2)}, u32[]{:S(2)}) %collective-permute-start.17) | collective-permute-done | bytes 524320 | tf_op jit(solution)/shard_map/ppermute | solution.py:20
  87.4 3.1 %collective-permute-start.21 = (f32[512,256]{1,0:T(8,128)S(1)}, f32[512,256]{1,0:T(8,128)S(1)}, u32[]{:S(2)}, u32[]{:S(2)}) collective-permute-start(f32[512,256]{1,0:T(8,128)S(1)} %shard_map.79), channel_id=1, source_target_pairs={{0,6},{1,7},{2,4},{3,5},{4,2},{5,3},{6,0},{7,1},{8,14},{9,15},{10,... | collective-permute-start | bytes 1572872 | tf_op jit(solution)/shard_map/ppermute | solution.py:20
  91.6 2.0 %collective-permute-start.20 = (f32[512,256]{1,0:T(8,128)S(1)}, f32[512,256]{1,0:T(8,128)S(1)}, u32[]{:S(2)}, u32[]{:S(2)}) collective-permute-start(f32[512,256]{1,0:T(8,128)S(1)} %shard_map.80.a), channel_id=1, source_target_pairs={{0,8},{1,9},{2,10},{3,11},{4,12},{5,13},{6,14},{7,15},{8,0},{9,1},... | collective-permute-start | bytes 1572872 | tf_op jit(solution)/shard_map/ppermute | solution.py:20
  95.8 1.8 %collective-permute-done.22.a.b = f32[512,256]{1,0:T(8,128)S(1)} collective-permute-done((f32[512,256]{1,0:T(8,128)S(1)}, f32[512,256]{1,0:T(8,128)S(1)}, u32[]{:S(2)}, u32[]{:S(2)}) %collective-permute-start.22) | collective-permute-done | bytes 524320 | tf_op jit(solution)/shard_map/ppermute | solution.py:20
  98.2 3.1 %collective-permute-start.26 = (f32[512,256]{1,0:T(8,128)S(1)}, f32[512,256]{1,0:T(8,128)S(1)}, u32[]{:S(2)}, u32[]{:S(2)}) collective-permute-start(f32[512,256]{1,0:T(8,128)S(1)} %shard_map.83), channel_id=1, source_target_pairs={{0,6},{1,7},{2,4},{3,5},{4,2},{5,3},{6,0},{7,1},{8,14},{9,15},{10,... | collective-permute-start | bytes 1572872 | tf_op jit(solution)/shard_map/ppermute | solution.py:20
  107.1 1.7 %collective-permute-start.23 = (f32[128,256]{1,0:T(8,128)S(1)}, f32[128,256]{1,0:T(8,128)S(1)}, u32[]{:S(2)}, u32[]{:S(2)}) collective-permute-start(f32[128,256]{1,0:T(8,128)S(1)} %slice_select_fusion.7), channel_id=1, source_target_pairs={{0,192},{64,128},{128,64},{192,0},{1,193},{65,129},{129,65},{193,1... | collective-permute-start | bytes 393224 | tf_op jit(solution)/shard_map/ppermute | solution.py:20
  108.8 4.5 %collective-permute-done.26.b = f32[512,256]{1,0:T(8,128)S(1)} collective-permute-done((f32[512,256]{1,0:T(8,128)S(1)}, f32[512,256]{1,0:T(8,128)S(1)}, u32[]{:S(2)}, u32[]{:S(2)}) %collective-permute-start.26) | collective-permute-done | bytes 524320 | tf_op jit(solution)/shard_map/ppermute | solution.py:20
  113.9 2.0 %collective-permute-start.29 = (f32[512,256]{1,0:T(8,128)S(1)}, f32[512,256]{1,0:T(8,128)S(1)}, u32[]{:S(2)}, u32[]{:S(2)}) collective-permute-start(f32[512,256]{1,0:T(8,128)S(1)} %shard_map.87.a), channel_id=1, source_target_pairs={{0,8},{1,9},{2,10},{3,11},{4,12},{5,13},{6,14},{7,15},{8,0},{9,1},... | collective-permute-start | bytes 1572872 | tf_op jit(solution)/shard_map/ppermute | solution.py:20
  119.5 7.9 %collective-permute-done.29.b = f32[512,256]{1,0:T(8,128)S(1)} collective-permute-done((f32[512,256]{1,0:T(8,128)S(1)}, f32[512,256]{1,0:T(8,128)S(1)}, u32[]{:S(2)}, u32[]{:S(2)}) %collective-permute-start.29) | collective-permute-done | bytes 524320 | tf_op jit(solution)/shard_map/ppermute | solution.py:20
  130.5 4.4 %collective-permute-done.31 = f32[256,256]{1,0:T(8,128)S(1)} collective-permute-done((f32[256,256]{1,0:T(8,128)S(1)}, f32[256,256]{1,0:T(8,128)S(1)}, u32[]{:S(2)}, u32[]{:S(2)}) %collective-permute-start.31) | collective-permute-done | bytes 262176 | tf_op jit(solution)/shard_map/ppermute | solution.py:20
  135.0 1.6 %collective-permute-start.32 = (f32[128,256]{1,0:T(8,128)S(1)}, f32[128,256]{1,0:T(8,128)S(1)}, u32[]{:S(2)}, u32[]{:S(2)}) collective-permute-start(f32[128,256]{1,0:T(8,128)S(1)} %slice_select_fusion.4), channel_id=1, source_target_pairs={{0,192},{64,128},{128,64},{192,0},{1,193},{65,129},{129,65},{193,1... | collective-permute-start | bytes 393224 | tf_op jit(solution)/shard_map/ppermute | solution.py:20
  137.3 4.0 %collective-permute-done.32 = f32[128,256]{1,0:T(8,128)S(1)} collective-permute-done((f32[128,256]{1,0:T(8,128)S(1)}, f32[128,256]{1,0:T(8,128)S(1)}, u32[]{:S(2)}, u32[]{:S(2)}) %collective-permute-start.32) | collective-permute-done | bytes 131104 | tf_op jit(solution)/shard_map/ppermute | solution.py:20
  (97 shorter events, 40.9 us)
Async XLA Ops:
  8.4 14.9 %collective-permute-start = (f32[512,256]{1,0:T(8,128)S(1)}, f32[512,256]{1,0:T(8,128)S(1)}, u32[]{:S(2)}, u32[]{:S(2)}) collective-permute-start(f32[512,256]{1,0:T(8,128)S(1)} %shard_map.64), channel_id=1, source_target_pairs={{0,64},{64,0},{128,192},{192,128},{1,65},{65,1},{129,193},{193,129... | collective-permute-start | bytes 1572872 | tf_op jit(solution)/shard_map/ppermute | solution.py:20
  11.5 23.0 %collective-permute-start.2 = (f32[512,256]{1,0:T(8,128)S(1)}, f32[512,256]{1,0:T(8,128)S(1)}, u32[]{:S(2)}, u32[]{:S(2)}) collective-permute-start(f32[512,256]{1,0:T(8,128)S(1)} %shard_map.65), channel_id=1, source_target_pairs={{0,64},{64,0},{128,192},{192,128},{1,65},{65,1},{129,193},{193,129... | collective-permute-start | bytes 1572872 | tf_op jit(solution)/shard_map/ppermute | solution.py:20
  13.8 31.9 %collective-permute-start.5 = (f32[512,256]{1,0:T(8,128)S(1)}, f32[512,256]{1,0:T(8,128)S(1)}, u32[]{:S(2)}, u32[]{:S(2)}) collective-permute-start(f32[512,256]{1,0:T(8,128)S(1)} %shard_map.66), channel_id=1, source_target_pairs={{0,64},{64,0},{128,192},{192,128},{1,65},{65,1},{129,193},{193,129... | collective-permute-start | bytes 1572872 | tf_op jit(solution)/shard_map/ppermute | solution.py:20
  17.0 38.8 %collective-permute-start.9 = (f32[512,256]{1,0:T(8,128)S(1)}, f32[512,256]{1,0:T(8,128)S(1)}, u32[]{:S(2)}, u32[]{:S(2)}) collective-permute-start(f32[512,256]{1,0:T(8,128)S(1)} %shard_map.67), channel_id=1, source_target_pairs={{0,64},{64,0},{128,192},{192,128},{1,65},{65,1},{129,193},{193,129... | collective-permute-start | bytes 1572872 | tf_op jit(solution)/shard_map/ppermute | solution.py:20
  23.3 14.1 %collective-permute-start.1 = (f32[512,256]{1,0:T(8,128)S(1)}, f32[512,256]{1,0:T(8,128)S(1)}, u32[]{:S(2)}, u32[]{:S(2)}) collective-permute-start(f32[512,256]{1,0:T(8,128)S(1)} %broadcast_select_fusion.3), channel_id=1, source_target_pairs={{0,192},{64,128},{128,64},{192,0},{1,193},{65,129},{129,65},{193,1... | collective-permute-start | bytes 1572872 | tf_op jit(solution)/shard_map/ppermute | solution.py:20
  26.3 35.0 %collective-permute-start.10 = (f32[2,256,512]{2,1,0:T(8,128)S(1)}, f32[2,256,512]{2,1,0:T(8,128)S(1)}, u32[]{:S(2)}, u32[]{:S(2)}) collective-permute-start(f32[2,256,512]{2,1,0:T(8,128)S(1)} %slice_bitcast_fusion), channel_id=1, source_target_pairs={{0,2},{1,3},{2,0},{3,1},{4,6},{5,7},{6,4},{7,5},{8,10},{9,11},{10,... | collective-permute-start | bytes 3145736 | tf_op jit(solution)/shard_map/ppermute | solution.py:20
  34.6 14.1 %collective-permute-start.4 = (f32[512,256]{1,0:T(8,128)S(1)}, f32[512,256]{1,0:T(8,128)S(1)}, u32[]{:S(2)}, u32[]{:S(2)}) collective-permute-start(f32[512,256]{1,0:T(8,128)S(1)} %broadcast_select_fusion.2), channel_id=1, source_target_pairs={{0,192},{64,128},{128,64},{192,0},{1,193},{65,129},{129,65},{193,1... | collective-permute-start | bytes 1572872 | tf_op jit(solution)/shard_map/ppermute | solution.py:20
  37.5 11.3 %collective-permute-start.3 = (f32[512,256]{1,0:T(8,128)S(1)}, f32[512,256]{1,0:T(8,128)S(1)}, u32[]{:S(2)}, u32[]{:S(2)}) collective-permute-start(f32[512,256]{1,0:T(8,128)S(1)} %select_select_fusion.3.a), channel_id=1, source_target_pairs={{0,1},{1,0},{2,3},{3,2},{4,5},{5,4},{6,7},{7,6},{8,9},{9,8},{10,11... | collective-permute-start | bytes 1572872 | tf_op jit(solution)/shard_map/ppermute | solution.py:20
  45.8 12.9 %collective-permute-start.8 = (f32[512,256]{1,0:T(8,128)S(1)}, f32[512,256]{1,0:T(8,128)S(1)}, u32[]{:S(2)}, u32[]{:S(2)}) collective-permute-start(f32[512,256]{1,0:T(8,128)S(1)} %broadcast_select_fusion.1), channel_id=1, source_target_pairs={{0,192},{64,128},{128,64},{192,0},{1,193},{65,129},{129,65},{193,1... | collective-permute-start | bytes 1572872 | tf_op jit(solution)/shard_map/ppermute | solution.py:20
  48.8 10.2 %collective-permute-start.7 = (f32[512,256]{1,0:T(8,128)S(1)}, f32[512,256]{1,0:T(8,128)S(1)}, u32[]{:S(2)}, u32[]{:S(2)}) collective-permute-start(f32[512,256]{1,0:T(8,128)S(1)} %select_select_fusion.2.a), channel_id=1, source_target_pairs={{0,1},{1,0},{2,3},{3,2},{4,5},{5,4},{6,7},{7,6},{8,9},{9,8},{10,11... | collective-permute-start | bytes 1572872 | tf_op jit(solution)/shard_map/ppermute | solution.py:20
  49.5 14.8 %collective-permute-start.6 = (f32[512,256]{1,0:T(8,128)S(1)}, f32[512,256]{1,0:T(8,128)S(1)}, u32[]{:S(2)}, u32[]{:S(2)}) collective-permute-start(f32[512,256]{1,0:T(8,128)S(1)} %shard_map.69.a.b), channel_id=1, source_target_pairs={{0,2},{1,3},{2,0},{3,1},{4,6},{5,7},{6,4},{7,5},{8,10},{9,11},{10,... | collective-permute-start | bytes 1572872 | tf_op jit(solution)/shard_map/ppermute | solution.py:20
  55.9 14.1 %collective-permute-start.14 = (f32[512,256]{1,0:T(8,128)S(1)}, f32[512,256]{1,0:T(8,128)S(1)}, u32[]{:S(2)}, u32[]{:S(2)}) collective-permute-start(f32[512,256]{1,0:T(8,128)S(1)} %broadcast_select_fusion), channel_id=1, source_target_pairs={{0,192},{64,128},{128,64},{192,0},{1,193},{65,129},{129,65},{193,1... | collective-permute-start | bytes 1572872 | tf_op jit(solution)/shard_map/ppermute | solution.py:20
  58.8 11.3 %collective-permute-start.13 = (f32[512,256]{1,0:T(8,128)S(1)}, f32[512,256]{1,0:T(8,128)S(1)}, u32[]{:S(2)}, u32[]{:S(2)}) collective-permute-start(f32[512,256]{1,0:T(8,128)S(1)} %select_select_fusion.1.a), channel_id=1, source_target_pairs={{0,1},{1,0},{2,3},{3,2},{4,5},{5,4},{6,7},{7,6},{8,9},{9,8},{10,11... | collective-permute-start | bytes 1572872 | tf_op jit(solution)/shard_map/ppermute | solution.py:20
  59.6 16.0 %collective-permute-start.12 = (f32[512,256]{1,0:T(8,128)S(1)}, f32[512,256]{1,0:T(8,128)S(1)}, u32[]{:S(2)}, u32[]{:S(2)}) collective-permute-start(f32[512,256]{1,0:T(8,128)S(1)} %shard_map.70.b.a), channel_id=1, source_target_pairs={{0,2},{1,3},{2,0},{3,1},{4,6},{5,7},{6,4},{7,5},{8,10},{9,11},{10,... | collective-permute-start | bytes 1572872 | tf_op jit(solution)/shard_map/ppermute | solution.py:20
  64.9 15.0 %collective-permute-start.11 = (f32[512,256]{1,0:T(8,128)S(1)}, f32[512,256]{1,0:T(8,128)S(1)}, u32[]{:S(2)}, u32[]{:S(2)}) collective-permute-start(f32[512,256]{1,0:T(8,128)S(1)} %shard_map.73), channel_id=1, source_target_pairs={{0,6},{1,7},{2,4},{3,5},{4,2},{5,3},{6,0},{7,1},{8,14},{9,15},{10,... | collective-permute-start | bytes 1572872 | tf_op jit(solution)/shard_map/ppermute | solution.py:20
  70.1 13.1 %collective-permute-start.18 = (f32[512,256]{1,0:T(8,128)S(1)}, f32[512,256]{1,0:T(8,128)S(1)}, u32[]{:S(2)}, u32[]{:S(2)}) collective-permute-start(f32[512,256]{1,0:T(8,128)S(1)} %select_select_fusion.a), channel_id=1, source_target_pairs={{0,1},{1,0},{2,3},{3,2},{4,5},{5,4},{6,7},{7,6},{8,9},{9,8},{10,11... | collective-permute-start | bytes 1572872 | tf_op jit(solution)/shard_map/ppermute | solution.py:20
  70.8 16.0 %collective-permute-start.17 = (f32[512,256]{1,0:T(8,128)S(1)}, f32[512,256]{1,0:T(8,128)S(1)}, u32[]{:S(2)}, u32[]{:S(2)}) collective-permute-start(f32[512,256]{1,0:T(8,128)S(1)} %shard_map.74.b.a), channel_id=1, source_target_pairs={{0,2},{1,3},{2,0},{3,1},{4,6},{5,7},{6,4},{7,5},{8,10},{9,11},{10,... | collective-permute-start | bytes 1572872 | tf_op jit(solution)/shard_map/ppermute | solution.py:20
  76.2 14.8 %collective-permute-start.16 = (f32[512,256]{1,0:T(8,128)S(1)}, f32[512,256]{1,0:T(8,128)S(1)}, u32[]{:S(2)}, u32[]{:S(2)}) collective-permute-start(f32[512,256]{1,0:T(8,128)S(1)} %shard_map.75), channel_id=1, source_target_pairs={{0,6},{1,7},{2,4},{3,5},{4,2},{5,3},{6,0},{7,1},{8,14},{9,15},{10,... | collective-permute-start | bytes 1572872 | tf_op jit(solution)/shard_map/ppermute | solution.py:20
  80.5 13.7 %collective-permute-start.15 = (f32[512,256]{1,0:T(8,128)S(1)}, f32[512,256]{1,0:T(8,128)S(1)}, u32[]{:S(2)}, u32[]{:S(2)}) collective-permute-start(f32[512,256]{1,0:T(8,128)S(1)} %shard_map.76.a), channel_id=1, source_target_pairs={{0,8},{1,9},{2,10},{3,11},{4,12},{5,13},{6,14},{7,15},{8,0},{9,1},... | collective-permute-start | bytes 1572872 | tf_op jit(solution)/shard_map/ppermute | solution.py:20
  83.8 13.8 %collective-permute-start.22 = (f32[512,256]{1,0:T(8,128)S(1)}, f32[512,256]{1,0:T(8,128)S(1)}, u32[]{:S(2)}, u32[]{:S(2)}) collective-permute-start(f32[512,256]{1,0:T(8,128)S(1)} %shard_map.78.b.a), channel_id=1, source_target_pairs={{0,2},{1,3},{2,0},{3,1},{4,6},{5,7},{6,4},{7,5},{8,10},{9,11},{10,... | collective-permute-start | bytes 1572872 | tf_op jit(solution)/shard_map/ppermute | solution.py:20
  87.4 15.2 %collective-permute-start.21 = (f32[512,256]{1,0:T(8,128)S(1)}, f32[512,256]{1,0:T(8,128)S(1)}, u32[]{:S(2)}, u32[]{:S(2)}) collective-permute-start(f32[512,256]{1,0:T(8,128)S(1)} %shard_map.79), channel_id=1, source_target_pairs={{0,6},{1,7},{2,4},{3,5},{4,2},{5,3},{6,0},{7,1},{8,14},{9,15},{10,... | collective-permute-start | bytes 1572872 | tf_op jit(solution)/shard_map/ppermute | solution.py:20
  91.6 13.9 %collective-permute-start.20 = (f32[512,256]{1,0:T(8,128)S(1)}, f32[512,256]{1,0:T(8,128)S(1)}, u32[]{:S(2)}, u32[]{:S(2)}) collective-permute-start(f32[512,256]{1,0:T(8,128)S(1)} %shard_map.80.a), channel_id=1, source_target_pairs={{0,8},{1,9},{2,10},{3,11},{4,12},{5,13},{6,14},{7,15},{8,0},{9,1},... | collective-permute-start | bytes 1572872 | tf_op jit(solution)/shard_map/ppermute | solution.py:20
  94.9 12.2 %collective-permute-start.19 = (f32[256,256]{1,0:T(8,128)S(1)}, f32[256,256]{1,0:T(8,128)S(1)}, u32[]{:S(2)}, u32[]{:S(2)}) collective-permute-start(f32[256,256]{1,0:T(8,128)S(1)} %slice_select_fusion.3), channel_id=1, source_target_pairs={{0,64},{64,0},{128,192},{192,128},{1,65},{65,1},{129,193},{193,129... | collective-permute-start | bytes 786440 | tf_op jit(solution)/shard_map/ppermute | solution.py:20
  98.2 15.1 %collective-permute-start.26 = (f32[512,256]{1,0:T(8,128)S(1)}, f32[512,256]{1,0:T(8,128)S(1)}, u32[]{:S(2)}, u32[]{:S(2)}) collective-permute-start(f32[512,256]{1,0:T(8,128)S(1)} %shard_map.83), channel_id=1, source_target_pairs={{0,6},{1,7},{2,4},{3,5},{4,2},{5,3},{6,0},{7,1},{8,14},{9,15},{10,... | collective-permute-start | bytes 1572872 | tf_op jit(solution)/shard_map/ppermute | solution.py:20
  103.3 13.0 %collective-permute-start.25 = (f32[512,256]{1,0:T(8,128)S(1)}, f32[512,256]{1,0:T(8,128)S(1)}, u32[]{:S(2)}, u32[]{:S(2)}) collective-permute-start(f32[512,256]{1,0:T(8,128)S(1)} %shard_map.84.a), channel_id=1, source_target_pairs={{0,8},{1,9},{2,10},{3,11},{4,12},{5,13},{6,14},{7,15},{8,0},{9,1},... | collective-permute-start | bytes 1572872 | tf_op jit(solution)/shard_map/ppermute | solution.py:20
  106.8 10.5 %collective-permute-start.24 = (f32[256,256]{1,0:T(8,128)S(1)}, f32[256,256]{1,0:T(8,128)S(1)}, u32[]{:S(2)}, u32[]{:S(2)}) collective-permute-start(f32[256,256]{1,0:T(8,128)S(1)} %slice_select_fusion.2), channel_id=1, source_target_pairs={{0,64},{64,0},{128,192},{192,128},{1,65},{65,1},{129,193},{193,129... | collective-permute-start | bytes 786440 | tf_op jit(solution)/shard_map/ppermute | solution.py:20
  107.1 11.7 %collective-permute-start.23 = (f32[128,256]{1,0:T(8,128)S(1)}, f32[128,256]{1,0:T(8,128)S(1)}, u32[]{:S(2)}, u32[]{:S(2)}) collective-permute-start(f32[128,256]{1,0:T(8,128)S(1)} %slice_select_fusion.7), channel_id=1, source_target_pairs={{0,192},{64,128},{128,64},{192,0},{1,193},{65,129},{129,65},{193,1... | collective-permute-start | bytes 393224 | tf_op jit(solution)/shard_map/ppermute | solution.py:20
  113.9 13.4 %collective-permute-start.29 = (f32[512,256]{1,0:T(8,128)S(1)}, f32[512,256]{1,0:T(8,128)S(1)}, u32[]{:S(2)}, u32[]{:S(2)}) collective-permute-start(f32[512,256]{1,0:T(8,128)S(1)} %shard_map.87.a), channel_id=1, source_target_pairs={{0,8},{1,9},{2,10},{3,11},{4,12},{5,13},{6,14},{7,15},{8,0},{9,1},... | collective-permute-start | bytes 1572872 | tf_op jit(solution)/shard_map/ppermute | solution.py:20
  117.0 11.3 %collective-permute-start.28 = (f32[256,256]{1,0:T(8,128)S(1)}, f32[256,256]{1,0:T(8,128)S(1)}, u32[]{:S(2)}, u32[]{:S(2)}) collective-permute-start(f32[256,256]{1,0:T(8,128)S(1)} %slice_select_fusion.1), channel_id=1, source_target_pairs={{0,64},{64,0},{128,192},{192,128},{1,65},{65,1},{129,193},{193,129... | collective-permute-start | bytes 786440 | tf_op jit(solution)/shard_map/ppermute | solution.py:20
  117.4 12.5 %collective-permute-start.27 = (f32[128,256]{1,0:T(8,128)S(1)}, f32[128,256]{1,0:T(8,128)S(1)}, u32[]{:S(2)}, u32[]{:S(2)}) collective-permute-start(f32[128,256]{1,0:T(8,128)S(1)} %slice_select_fusion.6), channel_id=1, source_target_pairs={{0,192},{64,128},{128,64},{192,0},{1,193},{65,129},{129,65},{193,1... | collective-permute-start | bytes 393224 | tf_op jit(solution)/shard_map/ppermute | solution.py:20
  128.0 6.9 %collective-permute-start.31 = (f32[256,256]{1,0:T(8,128)S(1)}, f32[256,256]{1,0:T(8,128)S(1)}, u32[]{:S(2)}, u32[]{:S(2)}) collective-permute-start(f32[256,256]{1,0:T(8,128)S(1)} %slice_select_fusion), channel_id=1, source_target_pairs={{0,64},{64,0},{128,192},{192,128},{1,65},{65,1},{129,193},{193,129... | collective-permute-start | bytes 786440 | tf_op jit(solution)/shard_map/ppermute | solution.py:20
  128.4 8.2 %collective-permute-start.30 = (f32[128,256]{1,0:T(8,128)S(1)}, f32[128,256]{1,0:T(8,128)S(1)}, u32[]{:S(2)}, u32[]{:S(2)}) collective-permute-start(f32[128,256]{1,0:T(8,128)S(1)} %slice_select_fusion.5), channel_id=1, source_target_pairs={{0,192},{64,128},{128,64},{192,0},{1,193},{65,129},{129,65},{193,1... | collective-permute-start | bytes 393224 | tf_op jit(solution)/shard_map/ppermute | solution.py:20
  (6 other events, 41.1 us)

commit v2 on v1

--- a/solution.py
+++ b/solution.py
@@ -32,6 +32,31 @@
 def dot3(a, b, dims):
     (ah, al), (bh, bl) = a, b
     return dot(ah, bh, dims) + (dot(ah, bl, dims) + dot(al, bh, dims))
+
+
+def choose_kernel(leaf_map, out):
+    x = lax.axis_index("obs")
+    b = lax.axis_index("bfly")
+    at = lax.broadcasted_iota(jnp.int32, (1, leaf_map.shape[1]), 1)
+    turn = jnp.sum(jnp.where(at == b, leaf_map[0:1, :], 0), axis=1, keepdims=True)
+    turn = jnp.broadcast_to(turn, (1, out.shape[1]))
+    out[0:1, :] = turn ^ 2
+    out[1:2, :] = turn
+    out[2:3, :] = (x + turn) % 4 ^ x ^ 1
+    out[3:4, :] = jnp.zeros_like(turn) + (x ^ x >> 1) % 2
+    out[4:5, :] = jnp.zeros_like(turn) + x % 2
+
+
+def choose(leaf_map, width):
+    return pl.pallas_call(
+        choose_kernel,
+        grid=(1,),
+        in_specs=[pl.BlockSpec(leaf_map.shape, lambda i: (0, 0))],
+        out_specs=pl.BlockSpec((8, width), lambda i: (0, 0)),
+        out_shape=jax.ShapeDtypeStruct((8, width), jnp.int32),
+        compiler_params=pltpu.CompilerParams(vmem_limit_bytes=1 << 20),
+        cost_estimate=CHEAP,
+    )(leaf_map)
 
 
 def project_kernel(block, basis, out, high, low):
@@ -112,21 +137,11 @@
 
 def body(obs_field, observer_leaf_bases, transfer, src_basis, leaf_map, partner_perm):
     nodes, leaf, rank = observer_leaf_bases.shape
-    x = lax.axis_index("obs")
-    b = lax.axis_index("bfly")
-
-    wanted = leaf_map[x, b]
-    wanted_there = leaf_map[x ^ 3, b]
-    outer = jnp.where((x == 0) | (x == 3), 0, 1)
-    inner = x & 1
-    flags = (
-        wanted_there == (x ^ 1), wanted == x, wanted == (x ^ 1),
-        outer == 0, inner == 0,
-    )
-    flags, obs_field, transfer, partner_perm = lax.optimization_barrier(
-        (flags, obs_field, transfer, partner_perm)
-    )
-    pass_on, stays, from_near, outer, inner = flags
+    obs_field = pltpu.with_memory_space_constraint(obs_field, pltpu.HBM)
+    picks = choose(leaf_map, rank)
+
+    def where(k, a, b):
+        return jnp.where(picks[k : k + 1] == 0, a, b)
 
     mats_there = flipped(transfer[1], "bfly", 2)
     mats = prepare(transfer, partner_perm, 0)
@@ -136,9 +151,9 @@
         j, at, width = CHUNKS[n]
         own = project(obs_field, bases, j, at, width)
         near = yield own, flipped(own, "obs", 1)
-        sent = jnp.where(pass_on, near, own)
+        sent = where(0, near, own)
         far = yield sent, flipped(sent, "obs", 3)
-        c = jnp.where(stays, own, jnp.where(from_near, near, far))
+        c = where(1, own, where(2, near, far))
         p = yield c, flipped(c, "bfly", 1)
         c = step(c, p, mats, 0, j)
         p = yield c, flipped(c, "bfly", 2)
@@ -149,13 +164,13 @@
         p = yield c, flipped(c, "bfly", 8)
         c = step(c, p, mats, 3, j)
         top, end = c[: 2 * width], c[2 * width :]
-        sent = jnp.where(outer, end, top)
+        sent = where(3, end, top)
         got = yield sent, flipped(sent, "obs", 1)
-        c = jnp.where(outer, top, end) + got
+        c = where(3, top, end) + got
         top, end = c[:width], c[width:]
-        sent = jnp.where(inner, end, top)
+        sent = where(4, end, top)
         got = yield sent, flipped(sent, "obs", 3)
-        c = jnp.where(inner, top, end) + got
+        c = where(4, top, end) + got
         out = lax.dot_general(
             c, src_basis[j], NT, precision=lax.Precision.HIGHEST,
             preferred_element_type=jnp.float32,

time: 143 us -> 139 us (0.972)
  Pallas kernels: 21.8 us -> 27.5 us
  waiting for transfers between devices: 58.6 us -> 53.5 us
  local copies, waits for them, and re-layouts: 4.89 us -> 1.32 us
  between operations: 2.41 us -> 0.47 us
    pallas_call x4, Pallas kernels: 6.4 us -> 12.1 us  [project(): pl.pallas_call(project_kernel, grid=(4,), in_specs=[pl.BlockSpec((leaf, w...]
    ppermute x33, waiting for transfers between devices: 58.6 us -> 53.5 us  [flipped(): return lax.ppermute(block, axis, [(i, i ^ mask) for i in range(count)])]
    unnamed x10, local copies, waits for them, and re-layouts: 3.43 us -> 1.25 us
  transfers between devices with their start and end apart: 33 -> 33, of which waited for: 18 -> 19; matrix products, arithmetic and copies ran while one was open for 2% -> 2% of each run, Pallas kernels for 14% -> 18%
where the time goes in v2:
time: 139 us
  waiting for transfers between devices  53.5 us (38%)
  starting transfers between devices  51.2 us (37%)
  Pallas kernels  27.5 us (20%)
  matrix products  2.51 us (2%)
  other arithmetic  2.28 us (2%)
    ppermute x33, waiting for transfers between devices, flipped(): return lax.ppermute(block, axis, [(i, i ^ mask) for i in range(count)])  53.5 us
    ppermute x33, starting transfers between devices, flipped(): return lax.ppermute(block, axis, [(i, i ^ mask) for i in range(count)])  51.2 us
    pallas_call x20, Pallas kernels, step(): pl.pallas_call(step_kernel, grid=(1,), in_specs=[whole, whole, one, one],...  12.4 us
    pallas_call x4, Pallas kernels, project(): pl.pallas_call(project_kernel, grid=(4,), in_specs=[pl.BlockSpec((leaf, w...  12.1 us
    pallas_call x2, Pallas kernels, prepare(): pl.pallas_call(functools.partial(prepare_kernel, first), grid=(levels, no...  3.01 us
  transfers between devices with their start and end apart: 33, of which 19 were waited for; matrix products, arithmetic and copies ran while one was open for 2% of the time, Pallas kernels for 18%

profile of v2, /device:TPU:64, one launch (start us, length us, event | category | flops | bytes accessed | tf_op | source)
XLA Modules:
  0.0 138.8 jit_solution(8293640234183483194)
XLA Ops:
  1.2 3.0 %shard_map.65 = f32[512,256]{1,0:T(8,128)S(1)} custom-call(f32[1024,1024]{1,0:T(8,128)} %block.7, f32[2,512,256]{2,1,0:T(8,128)S(1)} %copy-done), custom_call_target="tpu_custom_call" | custom-call | tf_op jit(solution)/shard_map/pallas_call | solution.py:73
  5.8 3.0 %shard_map.66 = f32[512,256]{1,0:T(8,128)S(1)} custom-call(f32[1024,1024]{1,0:T(8,128)} %block.7, f32[2,512,256]{2,1,0:T(8,128)S(1)} %copy-done), custom_call_target="tpu_custom_call" | custom-call | tf_op jit(solution)/shard_map/pallas_call | solution.py:73
  9.5 3.0 %shard_map.67 = f32[512,256]{1,0:T(8,128)S(1)} custom-call(f32[1024,1024]{1,0:T(8,128)} %block.7, f32[2,512,256]{2,1,0:T(8,128)S(1)} %copy-done), custom_call_target="tpu_custom_call" | custom-call | tf_op jit(solution)/shard_map/pallas_call | solution.py:73
  14.1 3.0 %shard_map.68 = f32[512,256]{1,0:T(8,128)S(1)} custom-call(f32[1024,1024]{1,0:T(8,128)} %block.7, f32[2,512,256]{2,1,0:T(8,128)S(1)} %copy-done), custom_call_target="tpu_custom_call" | custom-call | tf_op jit(solution)/shard_map/pallas_call | solution.py:73
  19.3 2.8 %collective-permute-start.1 = (f32[512,256]{1,0:T(8,128)S(1)}, f32[512,256]{1,0:T(8,128)S(1)}, u32[]{:S(2)}, u32[]{:S(2)}) collective-permute-start(f32[512,256]{1,0:T(8,128)S(1)} %broadcast_select_fusion.3), channel_id=1, source_target_pairs={{0,192},{64,128},{128,64},{192,0},{1,193},{65,129},{129,65},{193,1... | collective-permute-start | bytes 1572872 | tf_op jit(solution)/shard_map/ppermute | solution.py:20
  22.2 1.7 %collective-permute-start.10 = (f32[2,256,512]{2,1,0:T(8,128)S(1)}, f32[2,256,512]{2,1,0:T(8,128)S(1)}, u32[]{:S(2)}, u32[]{:S(2)}) collective-permute-start(f32[2,256,512]{2,1,0:T(8,128)S(1)} %slice_bitcast_fusion), channel_id=1, source_target_pairs={{0,2},{1,3},{2,0},{3,1},{4,6},{5,7},{6,4},{7,5},{8,10},{9,11},{10,... | collective-permute-start | bytes 3145736 | tf_op jit(solution)/shard_map/ppermute | solution.py:20
  23.9 2.4 %shard_map.69 = (bf16[4,2,256,512]{3,2,1,0:T(8,128)(2,1)S(1)}, bf16[4,2,256,512]{3,2,1,0:T(8,128)(2,1)S(1)}) custom-call(s32[4,256]{1,0:T(4,128)S(1)} %copy-done.2, f32[4,2,256,512]{3,2,1,0:T(8,128)S(1)} %copy-done.1), custom_call_target="tpu_custom_call" | custom-call | tf_op jit(solution)/shard_map/pallas_call | solution.py:105
  26.3 4.1 %collective-permute-done.2 = f32[512,256]{1,0:T(8,128)S(1)} collective-permute-done((f32[512,256]{1,0:T(8,128)S(1)}, f32[512,256]{1,0:T(8,128)S(1)}, u32[]{:S(2)}, u32[]{:S(2)}) %collective-permute-start.2) | collective-permute-done | bytes 524320 | tf_op jit(solution)/shard_map/ppermute | solution.py:20
  30.5 2.8 %collective-permute-start.4 = (f32[512,256]{1,0:T(8,128)S(1)}, f32[512,256]{1,0:T(8,128)S(1)}, u32[]{:S(2)}, u32[]{:S(2)}) collective-permute-start(f32[512,256]{1,0:T(8,128)S(1)} %broadcast_select_fusion.2), channel_id=1, source_target_pairs={{0,192},{64,128},{128,64},{192,0},{1,193},{65,129},{129,65},{193,1... | collective-permute-start | bytes 1572872 | tf_op jit(solution)/shard_map/ppermute | solution.py:20
  33.5 8.1 %collective-permute-done.5 = f32[512,256]{1,0:T(8,128)S(1)} collective-permute-done((f32[512,256]{1,0:T(8,128)S(1)}, f32[512,256]{1,0:T(8,128)S(1)}, u32[]{:S(2)}, u32[]{:S(2)}) %collective-permute-start.5) | collective-permute-done | bytes 524320 | tf_op jit(solution)/shard_map/ppermute | solution.py:20
  41.7 2.8 %collective-permute-start.8 = (f32[512,256]{1,0:T(8,128)S(1)}, f32[512,256]{1,0:T(8,128)S(1)}, u32[]{:S(2)}, u32[]{:S(2)}) collective-permute-start(f32[512,256]{1,0:T(8,128)S(1)} %broadcast_select_fusion.1), channel_id=1, source_target_pairs={{0,192},{64,128},{128,64},{192,0},{1,193},{65,129},{129,65},{193,1... | collective-permute-start | bytes 1572872 | tf_op jit(solution)/shard_map/ppermute | solution.py:20
  45.4 1.7 %collective-permute-start.6 = (f32[512,256]{1,0:T(8,128)S(1)}, f32[512,256]{1,0:T(8,128)S(1)}, u32[]{:S(2)}, u32[]{:S(2)}) collective-permute-start(f32[512,256]{1,0:T(8,128)S(1)} %shard_map.70.a.b), channel_id=1, source_target_pairs={{0,2},{1,3},{2,0},{3,1},{4,6},{5,7},{6,4},{7,5},{8,10},{9,11},{10,... | collective-permute-start | bytes 1572872 | tf_op jit(solution)/shard_map/ppermute | solution.py:20
  47.1 4.7 %collective-permute-done.9 = f32[512,256]{1,0:T(8,128)S(1)} collective-permute-done((f32[512,256]{1,0:T(8,128)S(1)}, f32[512,256]{1,0:T(8,128)S(1)}, u32[]{:S(2)}, u32[]{:S(2)}) %collective-permute-start.9) | collective-permute-done | bytes 524320 | tf_op jit(solution)/shard_map/ppermute | solution.py:20
  51.8 2.8 %collective-permute-start.14 = (f32[512,256]{1,0:T(8,128)S(1)}, f32[512,256]{1,0:T(8,128)S(1)}, u32[]{:S(2)}, u32[]{:S(2)}) collective-permute-start(f32[512,256]{1,0:T(8,128)S(1)} %broadcast_select_fusion), channel_id=1, source_target_pairs={{0,192},{64,128},{128,64},{192,0},{1,193},{65,129},{129,65},{193,1... | collective-permute-start | bytes 1572872 | tf_op jit(solution)/shard_map/ppermute | solution.py:20
  57.8 2.4 %collective-permute-done.6.b.a = f32[512,256]{1,0:T(8,128)S(1)} collective-permute-done((f32[512,256]{1,0:T(8,128)S(1)}, f32[512,256]{1,0:T(8,128)S(1)}, u32[]{:S(2)}, u32[]{:S(2)}) %collective-permute-start.6) | collective-permute-done | bytes 524320 | tf_op jit(solution)/shard_map/ppermute | solution.py:20
  60.8 3.3 %collective-permute-start.11 = (f32[512,256]{1,0:T(8,128)S(1)}, f32[512,256]{1,0:T(8,128)S(1)}, u32[]{:S(2)}, u32[]{:S(2)}) collective-permute-start(f32[512,256]{1,0:T(8,128)S(1)} %shard_map.74), channel_id=1, source_target_pairs={{0,6},{1,7},{2,4},{3,5},{4,2},{5,3},{6,0},{7,1},{8,14},{9,15},{10,... | collective-permute-start | bytes 1572872 | tf_op jit(solution)/shard_map/ppermute | solution.py:20
  64.1 1.8 %collective-permute-done.14 = f32[512,256]{1,0:T(8,128)S(1)} collective-permute-done((f32[512,256]{1,0:T(8,128)S(1)}, f32[512,256]{1,0:T(8,128)S(1)}, u32[]{:S(2)}, u32[]{:S(2)}) %collective-permute-start.14) | collective-permute-done | bytes 524320 | tf_op jit(solution)/shard_map/ppermute | solution.py:20
  68.4 3.0 %collective-permute-done.12.a.b = f32[512,256]{1,0:T(8,128)S(1)} collective-permute-done((f32[512,256]{1,0:T(8,128)S(1)}, f32[512,256]{1,0:T(8,128)S(1)}, u32[]{:S(2)}, u32[]{:S(2)}) %collective-permute-start.12) | collective-permute-done | bytes 524320 | tf_op jit(solution)/shard_map/ppermute | solution.py:20
  72.1 3.1 %collective-permute-start.16 = (f32[512,256]{1,0:T(8,128)S(1)}, f32[512,256]{1,0:T(8,128)S(1)}, u32[]{:S(2)}, u32[]{:S(2)}) collective-permute-start(f32[512,256]{1,0:T(8,128)S(1)} %shard_map.76), channel_id=1, source_target_pairs={{0,6},{1,7},{2,4},{3,5},{4,2},{5,3},{6,0},{7,1},{8,14},{9,15},{10,... | collective-permute-start | bytes 1572872 | tf_op jit(solution)/shard_map/ppermute | solution.py:20
  76.4 2.0 %collective-permute-start.15 = (f32[512,256]{1,0:T(8,128)S(1)}, f32[512,256]{1,0:T(8,128)S(1)}, u32[]{:S(2)}, u32[]{:S(2)}) collective-permute-start(f32[512,256]{1,0:T(8,128)S(1)} %shard_map.77.a), channel_id=1, source_target_pairs={{0,8},{1,9},{2,10},{3,11},{4,12},{5,13},{6,14},{7,15},{8,0},{9,1},... | collective-permute-start | bytes 1572872 | tf_op jit(solution)/shard_map/ppermute | solution.py:20
  79.9 2.8 %collective-permute-done.17.a.b = f32[512,256]{1,0:T(8,128)S(1)} collective-permute-done((f32[512,256]{1,0:T(8,128)S(1)}, f32[512,256]{1,0:T(8,128)S(1)}, u32[]{:S(2)}, u32[]{:S(2)}) %collective-permute-start.17) | collective-permute-done | bytes 524320 | tf_op jit(solution)/shard_map/ppermute | solution.py:20
  83.3 3.1 %collective-permute-start.21 = (f32[512,256]{1,0:T(8,128)S(1)}, f32[512,256]{1,0:T(8,128)S(1)}, u32[]{:S(2)}, u32[]{:S(2)}) collective-permute-start(f32[512,256]{1,0:T(8,128)S(1)} %shard_map.80), channel_id=1, source_target_pairs={{0,6},{1,7},{2,4},{3,5},{4,2},{5,3},{6,0},{7,1},{8,14},{9,15},{10,... | collective-permute-start | bytes 1572872 | tf_op jit(solution)/shard_map/ppermute | solution.py:20
  87.5 2.0 %collective-permute-start.20 = (f32[512,256]{1,0:T(8,128)S(1)}, f32[512,256]{1,0:T(8,128)S(1)}, u32[]{:S(2)}, u32[]{:S(2)}) collective-permute-start(f32[512,256]{1,0:T(8,128)S(1)} %shard_map.81.a), channel_id=1, source_target_pairs={{0,8},{1,9},{2,10},{3,11},{4,12},{5,13},{6,14},{7,15},{8,0},{9,1},... | collective-permute-start | bytes 1572872 | tf_op jit(solution)/shard_map/ppermute | solution.py:20
  91.7 1.8 %collective-permute-done.22.a.b = f32[512,256]{1,0:T(8,128)S(1)} collective-permute-done((f32[512,256]{1,0:T(8,128)S(1)}, f32[512,256]{1,0:T(8,128)S(1)}, u32[]{:S(2)}, u32[]{:S(2)}) %collective-permute-start.22) | collective-permute-done | bytes 524320 | tf_op jit(solution)/shard_map/ppermute | solution.py:20
  94.1 3.1 %collective-permute-start.26 = (f32[512,256]{1,0:T(8,128)S(1)}, f32[512,256]{1,0:T(8,128)S(1)}, u32[]{:S(2)}, u32[]{:S(2)}) collective-permute-start(f32[512,256]{1,0:T(8,128)S(1)} %shard_map.84), channel_id=1, source_target_pairs={{0,6},{1,7},{2,4},{3,5},{4,2},{5,3},{6,0},{7,1},{8,14},{9,15},{10,... | collective-permute-start | bytes 1572872 | tf_op jit(solution)/shard_map/ppermute | solution.py:20
  103.0 1.8 %collective-permute-start.23 = (f32[128,256]{1,0:T(8,128)S(1)}, f32[128,256]{1,0:T(8,128)S(1)}, u32[]{:S(2)}, u32[]{:S(2)}) collective-permute-start(f32[128,256]{1,0:T(8,128)S(1)} %slice_select_fusion.7), channel_id=1, source_target_pairs={{0,192},{64,128},{128,64},{192,0},{1,193},{65,129},{129,65},{193,1... | collective-permute-start | bytes 393224 | tf_op jit(solution)/shard_map/ppermute | solution.py:20
  104.8 4.4 %collective-permute-done.26.b = f32[512,256]{1,0:T(8,128)S(1)} collective-permute-done((f32[512,256]{1,0:T(8,128)S(1)}, f32[512,256]{1,0:T(8,128)S(1)}, u32[]{:S(2)}, u32[]{:S(2)}) %collective-permute-start.26) | collective-permute-done | bytes 524320 | tf_op jit(solution)/shard_map/ppermute | solution.py:20
  109.8 2.0 %collective-permute-start.29 = (f32[512,256]{1,0:T(8,128)S(1)}, f32[512,256]{1,0:T(8,128)S(1)}, u32[]{:S(2)}, u32[]{:S(2)}) collective-permute-start(f32[512,256]{1,0:T(8,128)S(1)} %shard_map.88.a), channel_id=1, source_target_pairs={{0,8},{1,9},{2,10},{3,11},{4,12},{5,13},{6,14},{7,15},{8,0},{9,1},... | collective-permute-start | bytes 1572872 | tf_op jit(solution)/shard_map/ppermute | solution.py:20
  115.4 7.8 %collective-permute-done.29.b = f32[512,256]{1,0:T(8,128)S(1)} collective-permute-done((f32[512,256]{1,0:T(8,128)S(1)}, f32[512,256]{1,0:T(8,128)S(1)}, u32[]{:S(2)}, u32[]{:S(2)}) %collective-permute-start.29) | collective-permute-done | bytes 524320 | tf_op jit(solution)/shard_map/ppermute | solution.py:20
  126.5 4.3 %collective-permute-done.31 = f32[256,256]{1,0:T(8,128)S(1)} collective-permute-done((f32[256,256]{1,0:T(8,128)S(1)}, f32[256,256]{1,0:T(8,128)S(1)}, u32[]{:S(2)}, u32[]{:S(2)}) %collective-permute-start.31) | collective-permute-done | bytes 262176 | tf_op jit(solution)/shard_map/ppermute | solution.py:20
  130.9 1.7 %collective-permute-start.32 = (f32[128,256]{1,0:T(8,128)S(1)}, f32[128,256]{1,0:T(8,128)S(1)}, u32[]{:S(2)}, u32[]{:S(2)}) collective-permute-start(f32[128,256]{1,0:T(8,128)S(1)} %slice_select_fusion.4), channel_id=1, source_target_pairs={{0,192},{64,128},{128,64},{192,0},{1,193},{65,129},{129,65},{193,1... | collective-permute-start | bytes 393224 | tf_op jit(solution)/shard_map/ppermute | solution.py:20
  133.2 3.9 %collective-permute-done.32 = f32[128,256]{1,0:T(8,128)S(1)} collective-permute-done((f32[128,256]{1,0:T(8,128)S(1)}, f32[128,256]{1,0:T(8,128)S(1)}, u32[]{:S(2)}, u32[]{:S(2)}) %collective-permute-start.32) | collective-permute-done | bytes 131104 | tf_op jit(solution)/shard_map/ppermute | solution.py:20
  (98 shorter events, 38.1 us)
Async XLA Ops:
  4.2 14.9 %collective-permute-start = (f32[512,256]{1,0:T(8,128)S(1)}, f32[512,256]{1,0:T(8,128)S(1)}, u32[]{:S(2)}, u32[]{:S(2)}) collective-permute-start(f32[512,256]{1,0:T(8,128)S(1)} %shard_map.65), channel_id=1, source_target_pairs={{0,64},{64,0},{128,192},{192,128},{1,65},{65,1},{129,193},{193,129... | collective-permute-start | bytes 1572872 | tf_op jit(solution)/shard_map/ppermute | solution.py:20
  8.8 21.5 %collective-permute-start.2 = (f32[512,256]{1,0:T(8,128)S(1)}, f32[512,256]{1,0:T(8,128)S(1)}, u32[]{:S(2)}, u32[]{:S(2)}) collective-permute-start(f32[512,256]{1,0:T(8,128)S(1)} %shard_map.66), channel_id=1, source_target_pairs={{0,64},{64,0},{128,192},{192,128},{1,65},{65,1},{129,193},{193,129... | collective-permute-start | bytes 1572872 | tf_op jit(solution)/shard_map/ppermute | solution.py:20
  12.5 29.1 %collective-permute-start.5 = (f32[512,256]{1,0:T(8,128)S(1)}, f32[512,256]{1,0:T(8,128)S(1)}, u32[]{:S(2)}, u32[]{:S(2)}) collective-permute-start(f32[512,256]{1,0:T(8,128)S(1)} %shard_map.67), channel_id=1, source_target_pairs={{0,64},{64,0},{128,192},{192,128},{1,65},{65,1},{129,193},{193,129... | collective-permute-start | bytes 1572872 | tf_op jit(solution)/shard_map/ppermute | solution.py:20
  17.1 34.6 %collective-permute-start.9 = (f32[512,256]{1,0:T(8,128)S(1)}, f32[512,256]{1,0:T(8,128)S(1)}, u32[]{:S(2)}, u32[]{:S(2)}) collective-permute-start(f32[512,256]{1,0:T(8,128)S(1)} %shard_map.68), channel_id=1, source_target_pairs={{0,64},{64,0},{128,192},{192,128},{1,65},{65,1},{129,193},{193,129... | collective-permute-start | bytes 1572872 | tf_op jit(solution)/shard_map/ppermute | solution.py:20
  19.3 14.0 %collective-permute-start.1 = (f32[512,256]{1,0:T(8,128)S(1)}, f32[512,256]{1,0:T(8,128)S(1)}, u32[]{:S(2)}, u32[]{:S(2)}) collective-permute-start(f32[512,256]{1,0:T(8,128)S(1)} %broadcast_select_fusion.3), channel_id=1, source_target_pairs={{0,192},{64,128},{128,64},{192,0},{1,193},{65,129},{129,65},{193,1... | collective-permute-start | bytes 1572872 | tf_op jit(solution)/shard_map/ppermute | solution.py:20
  22.2 35.0 %collective-permute-start.10 = (f32[2,256,512]{2,1,0:T(8,128)S(1)}, f32[2,256,512]{2,1,0:T(8,128)S(1)}, u32[]{:S(2)}, u32[]{:S(2)}) collective-permute-start(f32[2,256,512]{2,1,0:T(8,128)S(1)} %slice_bitcast_fusion), channel_id=1, source_target_pairs={{0,2},{1,3},{2,0},{3,1},{4,6},{5,7},{6,4},{7,5},{8,10},{9,11},{10,... | collective-permute-start | bytes 3145736 | tf_op jit(solution)/shard_map/ppermute | solution.py:20
  30.5 14.1 %collective-permute-start.4 = (f32[512,256]{1,0:T(8,128)S(1)}, f32[512,256]{1,0:T(8,128)S(1)}, u32[]{:S(2)}, u32[]{:S(2)}) collective-permute-start(f32[512,256]{1,0:T(8,128)S(1)} %broadcast_select_fusion.2), channel_id=1, source_target_pairs={{0,192},{64,128},{128,64},{192,0},{1,193},{65,129},{129,65},{193,1... | collective-permute-start | bytes 1572872 | tf_op jit(solution)/shard_map/ppermute | solution.py:20
  33.4 11.3 %collective-permute-start.3 = (f32[512,256]{1,0:T(8,128)S(1)}, f32[512,256]{1,0:T(8,128)S(1)}, u32[]{:S(2)}, u32[]{:S(2)}) collective-permute-start(f32[512,256]{1,0:T(8,128)S(1)} %select_select_fusion.3.a), channel_id=1, source_target_pairs={{0,1},{1,0},{2,3},{3,2},{4,5},{5,4},{6,7},{7,6},{8,9},{9,8},{10,11... | collective-permute-start | bytes 1572872 | tf_op jit(solution)/shard_map/ppermute | solution.py:20
  41.7 13.0 %collective-permute-start.8 = (f32[512,256]{1,0:T(8,128)S(1)}, f32[512,256]{1,0:T(8,128)S(1)}, u32[]{:S(2)}, u32[]{:S(2)}) collective-permute-start(f32[512,256]{1,0:T(8,128)S(1)} %broadcast_select_fusion.1), channel_id=1, source_target_pairs={{0,192},{64,128},{128,64},{192,0},{1,193},{65,129},{129,65},{193,1... | collective-permute-start | bytes 1572872 | tf_op jit(solution)/shard_map/ppermute | solution.py:20
  44.7 10.2 %collective-permute-start.7 = (f32[512,256]{1,0:T(8,128)S(1)}, f32[512,256]{1,0:T(8,128)S(1)}, u32[]{:S(2)}, u32[]{:S(2)}) collective-permute-start(f32[512,256]{1,0:T(8,128)S(1)} %select_select_fusion.2.a), channel_id=1, source_target_pairs={{0,1},{1,0},{2,3},{3,2},{4,5},{5,4},{6,7},{7,6},{8,9},{9,8},{10,11... | collective-permute-start | bytes 1572872 | tf_op jit(solution)/shard_map/ppermute | solution.py:20
  45.4 14.8 %collective-permute-start.6 = (f32[512,256]{1,0:T(8,128)S(1)}, f32[512,256]{1,0:T(8,128)S(1)}, u32[]{:S(2)}, u32[]{:S(2)}) collective-permute-start(f32[512,256]{1,0:T(8,128)S(1)} %shard_map.70.a.b), channel_id=1, source_target_pairs={{0,2},{1,3},{2,0},{3,1},{4,6},{5,7},{6,4},{7,5},{8,10},{9,11},{10,... | collective-permute-start | bytes 1572872 | tf_op jit(solution)/shard_map/ppermute | solution.py:20
  51.8 14.1 %collective-permute-start.14 = (f32[512,256]{1,0:T(8,128)S(1)}, f32[512,256]{1,0:T(8,128)S(1)}, u32[]{:S(2)}, u32[]{:S(2)}) collective-permute-start(f32[512,256]{1,0:T(8,128)S(1)} %broadcast_select_fusion), channel_id=1, source_target_pairs={{0,192},{64,128},{128,64},{192,0},{1,193},{65,129},{129,65},{193,1... | collective-permute-start | bytes 1572872 | tf_op jit(solution)/shard_map/ppermute | solution.py:20
  54.8 11.3 %collective-permute-start.13 = (f32[512,256]{1,0:T(8,128)S(1)}, f32[512,256]{1,0:T(8,128)S(1)}, u32[]{:S(2)}, u32[]{:S(2)}) collective-permute-start(f32[512,256]{1,0:T(8,128)S(1)} %select_select_fusion.1.a), channel_id=1, source_target_pairs={{0,1},{1,0},{2,3},{3,2},{4,5},{5,4},{6,7},{7,6},{8,9},{9,8},{10,11... | collective-permute-start | bytes 1572872 | tf_op jit(solution)/shard_map/ppermute | solution.py:20
  55.5 15.9 %collective-permute-start.12 = (f32[512,256]{1,0:T(8,128)S(1)}, f32[512,256]{1,0:T(8,128)S(1)}, u32[]{:S(2)}, u32[]{:S(2)}) collective-permute-start(f32[512,256]{1,0:T(8,128)S(1)} %shard_map.71.b.a), channel_id=1, source_target_pairs={{0,2},{1,3},{2,0},{3,1},{4,6},{5,7},{6,4},{7,5},{8,10},{9,11},{10,... | collective-permute-start | bytes 1572872 | tf_op jit(solution)/shard_map/ppermute | solution.py:20
  60.8 14.9 %collective-permute-start.11 = (f32[512,256]{1,0:T(8,128)S(1)}, f32[512,256]{1,0:T(8,128)S(1)}, u32[]{:S(2)}, u32[]{:S(2)}) collective-permute-start(f32[512,256]{1,0:T(8,128)S(1)} %shard_map.74), channel_id=1, source_target_pairs={{0,6},{1,7},{2,4},{3,5},{4,2},{5,3},{6,0},{7,1},{8,14},{9,15},{10,... | collective-permute-start | bytes 1572872 | tf_op jit(solution)/shard_map/ppermute | solution.py:20
  66.0 13.0 %collective-permute-start.18 = (f32[512,256]{1,0:T(8,128)S(1)}, f32[512,256]{1,0:T(8,128)S(1)}, u32[]{:S(2)}, u32[]{:S(2)}) collective-permute-start(f32[512,256]{1,0:T(8,128)S(1)} %select_select_fusion.a), channel_id=1, source_target_pairs={{0,1},{1,0},{2,3},{3,2},{4,5},{5,4},{6,7},{7,6},{8,9},{9,8},{10,11... | collective-permute-start | bytes 1572872 | tf_op jit(solution)/shard_map/ppermute | solution.py:20
  66.8 15.9 %collective-permute-start.17 = (f32[512,256]{1,0:T(8,128)S(1)}, f32[512,256]{1,0:T(8,128)S(1)}, u32[]{:S(2)}, u32[]{:S(2)}) collective-permute-start(f32[512,256]{1,0:T(8,128)S(1)} %shard_map.75.b.a), channel_id=1, source_target_pairs={{0,2},{1,3},{2,0},{3,1},{4,6},{5,7},{6,4},{7,5},{8,10},{9,11},{10,... | collective-permute-start | bytes 1572872 | tf_op jit(solution)/shard_map/ppermute | solution.py:20
  72.1 14.8 %collective-permute-start.16 = (f32[512,256]{1,0:T(8,128)S(1)}, f32[512,256]{1,0:T(8,128)S(1)}, u32[]{:S(2)}, u32[]{:S(2)}) collective-permute-start(f32[512,256]{1,0:T(8,128)S(1)} %shard_map.76), channel_id=1, source_target_pairs={{0,6},{1,7},{2,4},{3,5},{4,2},{5,3},{6,0},{7,1},{8,14},{9,15},{10,... | collective-permute-start | bytes 1572872 | tf_op jit(solution)/shard_map/ppermute | solution.py:20
  76.4 13.7 %collective-permute-start.15 = (f32[512,256]{1,0:T(8,128)S(1)}, f32[512,256]{1,0:T(8,128)S(1)}, u32[]{:S(2)}, u32[]{:S(2)}) collective-permute-start(f32[512,256]{1,0:T(8,128)S(1)} %shard_map.77.a), channel_id=1, source_target_pairs={{0,8},{1,9},{2,10},{3,11},{4,12},{5,13},{6,14},{7,15},{8,0},{9,1},... | collective-permute-start | bytes 1572872 | tf_op jit(solution)/shard_map/ppermute | solution.py:20
  79.7 13.8 %collective-permute-start.22 = (f32[512,256]{1,0:T(8,128)S(1)}, f32[512,256]{1,0:T(8,128)S(1)}, u32[]{:S(2)}, u32[]{:S(2)}) collective-permute-start(f32[512,256]{1,0:T(8,128)S(1)} %shard_map.79.b.a), channel_id=1, source_target_pairs={{0,2},{1,3},{2,0},{3,1},{4,6},{5,7},{6,4},{7,5},{8,10},{9,11},{10,... | collective-permute-start | bytes 1572872 | tf_op jit(solution)/shard_map/ppermute | solution.py:20
  83.3 15.3 %collective-permute-start.21 = (f32[512,256]{1,0:T(8,128)S(1)}, f32[512,256]{1,0:T(8,128)S(1)}, u32[]{:S(2)}, u32[]{:S(2)}) collective-permute-start(f32[512,256]{1,0:T(8,128)S(1)} %shard_map.80), channel_id=1, source_target_pairs={{0,6},{1,7},{2,4},{3,5},{4,2},{5,3},{6,0},{7,1},{8,14},{9,15},{10,... | collective-permute-start | bytes 1572872 | tf_op jit(solution)/shard_map/ppermute | solution.py:20
  87.5 13.9 %collective-permute-start.20 = (f32[512,256]{1,0:T(8,128)S(1)}, f32[512,256]{1,0:T(8,128)S(1)}, u32[]{:S(2)}, u32[]{:S(2)}) collective-permute-start(f32[512,256]{1,0:T(8,128)S(1)} %shard_map.81.a), channel_id=1, source_target_pairs={{0,8},{1,9},{2,10},{3,11},{4,12},{5,13},{6,14},{7,15},{8,0},{9,1},... | collective-permute-start | bytes 1572872 | tf_op jit(solution)/shard_map/ppermute | solution.py:20
  90.8 12.2 %collective-permute-start.19 = (f32[256,256]{1,0:T(8,128)S(1)}, f32[256,256]{1,0:T(8,128)S(1)}, u32[]{:S(2)}, u32[]{:S(2)}) collective-permute-start(f32[256,256]{1,0:T(8,128)S(1)} %slice_select_fusion.3), channel_id=1, source_target_pairs={{0,64},{64,0},{128,192},{192,128},{1,65},{65,1},{129,193},{193,129... | collective-permute-start | bytes 786440 | tf_op jit(solution)/shard_map/ppermute | solution.py:20
  94.1 15.1 %collective-permute-start.26 = (f32[512,256]{1,0:T(8,128)S(1)}, f32[512,256]{1,0:T(8,128)S(1)}, u32[]{:S(2)}, u32[]{:S(2)}) collective-permute-start(f32[512,256]{1,0:T(8,128)S(1)} %shard_map.84), channel_id=1, source_target_pairs={{0,6},{1,7},{2,4},{3,5},{4,2},{5,3},{6,0},{7,1},{8,14},{9,15},{10,... | collective-permute-start | bytes 1572872 | tf_op jit(solution)/shard_map/ppermute | solution.py:20
  99.2 13.0 %collective-permute-start.25 = (f32[512,256]{1,0:T(8,128)S(1)}, f32[512,256]{1,0:T(8,128)S(1)}, u32[]{:S(2)}, u32[]{:S(2)}) collective-permute-start(f32[512,256]{1,0:T(8,128)S(1)} %shard_map.85.a), channel_id=1, source_target_pairs={{0,8},{1,9},{2,10},{3,11},{4,12},{5,13},{6,14},{7,15},{8,0},{9,1},... | collective-permute-start | bytes 1572872 | tf_op jit(solution)/shard_map/ppermute | solution.py:20
  102.6 10.5 %collective-permute-start.24 = (f32[256,256]{1,0:T(8,128)S(1)}, f32[256,256]{1,0:T(8,128)S(1)}, u32[]{:S(2)}, u32[]{:S(2)}) collective-permute-start(f32[256,256]{1,0:T(8,128)S(1)} %slice_select_fusion.2), channel_id=1, source_target_pairs={{0,64},{64,0},{128,192},{192,128},{1,65},{65,1},{129,193},{193,129... | collective-permute-start | bytes 786440 | tf_op jit(solution)/shard_map/ppermute | solution.py:20
  103.0 11.8 %collective-permute-start.23 = (f32[128,256]{1,0:T(8,128)S(1)}, f32[128,256]{1,0:T(8,128)S(1)}, u32[]{:S(2)}, u32[]{:S(2)}) collective-permute-start(f32[128,256]{1,0:T(8,128)S(1)} %slice_select_fusion.7), channel_id=1, source_target_pairs={{0,192},{64,128},{128,64},{192,0},{1,193},{65,129},{129,65},{193,1... | collective-permute-start | bytes 393224 | tf_op jit(solution)/shard_map/ppermute | solution.py:20
  109.8 13.4 %collective-permute-start.29 = (f32[512,256]{1,0:T(8,128)S(1)}, f32[512,256]{1,0:T(8,128)S(1)}, u32[]{:S(2)}, u32[]{:S(2)}) collective-permute-start(f32[512,256]{1,0:T(8,128)S(1)} %shard_map.88.a), channel_id=1, source_target_pairs={{0,8},{1,9},{2,10},{3,11},{4,12},{5,13},{6,14},{7,15},{8,0},{9,1},... | collective-permute-start | bytes 1572872 | tf_op jit(solution)/shard_map/ppermute | solution.py:20
  112.9 11.4 %collective-permute-start.28 = (f32[256,256]{1,0:T(8,128)S(1)}, f32[256,256]{1,0:T(8,128)S(1)}, u32[]{:S(2)}, u32[]{:S(2)}) collective-permute-start(f32[256,256]{1,0:T(8,128)S(1)} %slice_select_fusion.1), channel_id=1, source_target_pairs={{0,64},{64,0},{128,192},{192,128},{1,65},{65,1},{129,193},{193,129... | collective-permute-start | bytes 786440 | tf_op jit(solution)/shard_map/ppermute | solution.py:20
  113.2 12.6 %collective-permute-start.27 = (f32[128,256]{1,0:T(8,128)S(1)}, f32[128,256]{1,0:T(8,128)S(1)}, u32[]{:S(2)}, u32[]{:S(2)}) collective-permute-start(f32[128,256]{1,0:T(8,128)S(1)} %slice_select_fusion.6), channel_id=1, source_target_pairs={{0,192},{64,128},{128,64},{192,0},{1,193},{65,129},{129,65},{193,1... | collective-permute-start | bytes 393224 | tf_op jit(solution)/shard_map/ppermute | solution.py:20
  123.9 6.9 %collective-permute-start.31 = (f32[256,256]{1,0:T(8,128)S(1)}, f32[256,256]{1,0:T(8,128)S(1)}, u32[]{:S(2)}, u32[]{:S(2)}) collective-permute-start(f32[256,256]{1,0:T(8,128)S(1)} %slice_select_fusion), channel_id=1, source_target_pairs={{0,64},{64,0},{128,192},{192,128},{1,65},{65,1},{129,193},{193,129... | collective-permute-start | bytes 786440 | tf_op jit(solution)/shard_map/ppermute | solution.py:20
  124.3 8.3 %collective-permute-start.30 = (f32[128,256]{1,0:T(8,128)S(1)}, f32[128,256]{1,0:T(8,128)S(1)}, u32[]{:S(2)}, u32[]{:S(2)}) collective-permute-start(f32[128,256]{1,0:T(8,128)S(1)} %slice_select_fusion.5), channel_id=1, source_target_pairs={{0,192},{64,128},{128,64},{192,0},{1,193},{65,129},{129,65},{193,1... | collective-permute-start | bytes 393224 | tf_op jit(solution)/shard_map/ppermute | solution.py:20
  (6 other events, 39.0 us)

commit v3 on v2

--- a/solution.py
+++ b/solution.py
@@ -59,32 +59,33 @@
     )(leaf_map)
 
 
-def project_kernel(block, basis, out, high, low):
-    @pl.when(pl.program_id(0) == 0)
-    def _():
-        high[...], low[...] = halves(basis[0])
-
-    out[...] = dot3(halves(block[...]), (high[...], low[...]), TN)
+def project_kernel(*refs):
+    *blocks, basis, out = refs
+    width = blocks[0].shape[1]
+    split = halves(basis[0])
+    for i, block in enumerate(blocks):
+        out[i * width : (i + 1) * width, :] = dot3(halves(block[...]), split, TN)
 
 
 def project(obs_field, bases, node, at, width):
     nodes, leaf, rank = bases.shape
     share = obs_field.shape[1] // 4
+    bases = pltpu.with_memory_space_constraint(bases, pltpu.HBM)
+    columns = [
+        pl.BlockSpec(
+            (leaf, width), functools.partial(lambda k, i: (node, k), (q * share + at) // width)
+        )
+        for q in (0, 3, 2, 1)
+    ]
     return pl.pallas_call(
         project_kernel,
-        grid=(4,),
-        in_specs=[
-            pl.BlockSpec(
-                (leaf, width), lambda i: (node, (3 * i) % 4 * (share // width) + at // width)
-            ),
-            pl.BlockSpec((1, leaf, rank), lambda i: (node, 0, 0)),
-        ],
-        out_specs=pl.BlockSpec((width, rank), lambda i: (i, 0)),
+        grid=(1,),
+        in_specs=columns + [pl.BlockSpec((1, leaf, rank), lambda i: (node, 0, 0))],
+        out_specs=pl.BlockSpec((4 * width, rank), lambda i: (0, 0)),
         out_shape=jax.ShapeDtypeStruct((4 * width, rank), jnp.float32),
-        scratch_shapes=[pltpu.VMEM((leaf, rank), jnp.bfloat16)] * 2,
         compiler_params=pltpu.CompilerParams(vmem_limit_bytes=LIMIT),
         cost_estimate=CHEAP,
-    )(obs_field, bases)
+    )(*[obs_field] * 4, bases)
 
 
 def prepare_kernel(first, perm, mats, high, low):

time: 139 us -> 137 us (0.986)
  Pallas kernels: 27.5 us -> 23.5 us
  waiting for transfers between devices: 53.5 us -> 56.1 us
    pallas_call x4, Pallas kernels: 12.1 us -> 8.05 us  [project(): pl.pallas_call(project_kernel, grid=(1,), in_specs=columns + [pl.BlockSpe...]
    ppermute x33, waiting for transfers between devices: 53.5 us -> 56.1 us  [flipped(): return lax.ppermute(block, axis, [(i, i ^ mask) for i in range(count)])]
  transfers between devices with their start and end apart: 33 -> 33, of which waited for: 19 -> 18; matrix products, arithmetic and copies ran while one was open for 2% -> 2% of each run, Pallas kernels for 18% -> 16%
where the time goes in v3:
time: 137 us
  waiting for transfers between devices  56.1 us (41%)
  starting transfers between devices  51.9 us (38%)
  Pallas kernels  23.5 us (17%)
  matrix products  2.51 us (2%)
  other arithmetic  2.22 us (2%)
    ppermute x33, waiting for transfers between devices, flipped(): return lax.ppermute(block, axis, [(i, i ^ mask) for i in range(count)])  56.1 us
    ppermute x33, starting transfers between devices, flipped(): return lax.ppermute(block, axis, [(i, i ^ mask) for i in range(count)])  51.9 us
    pallas_call x20, Pallas kernels, step(): pl.pallas_call(step_kernel, grid=(1,), in_specs=[whole, whole, one, one],...  12.4 us
    pallas_call x4, Pallas kernels, project(): pl.pallas_call(project_kernel, grid=(1,), in_specs=columns + [pl.BlockSpe...  8.05 us
    pallas_call x2, Pallas kernels, prepare(): pl.pallas_call(functools.partial(prepare_kernel, first), grid=(levels, no...  3.01 us
  transfers between devices with their start and end apart: 33, of which 18 were waited for; matrix products, arithmetic and copies ran while one was open for 2% of the time, Pallas kernels for 16%

profile of v3, /device:TPU:64, one launch (start us, length us, event | category | flops | bytes accessed | tf_op | source)
XLA Modules:
  0.0 136.8 jit_solution(10394878126498870057)
XLA Ops:
  0.0 2.0 %shard_map.65 = f32[512,256]{1,0:T(8,128)S(1)} custom-call(f32[1024,1024]{1,0:T(8,128)} %refs_3_.7, f32[1024,1024]{1,0:T(8,128)} %refs_3_.7, f32[1024,1024]{1,0:T(8,128)} %refs_3_.7, f32[1024,1024]{1,0:T(8,128)} %refs_3_.7, f32[2,512,256]{2,1,0:T(8,128)} %refs_4_.4), custom_call_target="tpu_custom_call" | custom-call | tf_op jit(solution)/shard_map/pallas_call | solution.py:80
  3.6 2.0 %shard_map.66 = f32[512,256]{1,0:T(8,128)S(1)} custom-call(f32[1024,1024]{1,0:T(8,128)} %refs_3_.7, f32[1024,1024]{1,0:T(8,128)} %refs_3_.7, f32[1024,1024]{1,0:T(8,128)} %refs_3_.7, f32[1024,1024]{1,0:T(8,128)} %refs_3_.7, f32[2,512,256]{2,1,0:T(8,128)} %refs_4_.4), custom_call_target="tpu_custom_call" | custom-call | tf_op jit(solution)/shard_map/pallas_call | solution.py:80
  6.2 2.0 %shard_map.67 = f32[512,256]{1,0:T(8,128)S(1)} custom-call(f32[1024,1024]{1,0:T(8,128)} %refs_3_.7, f32[1024,1024]{1,0:T(8,128)} %refs_3_.7, f32[1024,1024]{1,0:T(8,128)} %refs_3_.7, f32[1024,1024]{1,0:T(8,128)} %refs_3_.7, f32[2,512,256]{2,1,0:T(8,128)} %refs_4_.4), custom_call_target="tpu_custom_call" | custom-call | tf_op jit(solution)/shard_map/pallas_call | solution.py:80
  9.9 2.0 %shard_map.68 = f32[512,256]{1,0:T(8,128)S(1)} custom-call(f32[1024,1024]{1,0:T(8,128)} %refs_3_.7, f32[1024,1024]{1,0:T(8,128)} %refs_3_.7, f32[1024,1024]{1,0:T(8,128)} %refs_3_.7, f32[1024,1024]{1,0:T(8,128)} %refs_3_.7, f32[2,512,256]{2,1,0:T(8,128)} %refs_4_.4), custom_call_target="tpu_custom_call" | custom-call | tf_op jit(solution)/shard_map/pallas_call | solution.py:80
  13.0 3.9 %collective-permute-done = f32[512,256]{1,0:T(8,128)S(1)} collective-permute-done((f32[512,256]{1,0:T(8,128)S(1)}, f32[512,256]{1,0:T(8,128)S(1)}, u32[]{:S(2)}, u32[]{:S(2)}) %collective-permute-start) | collective-permute-done | bytes 524320 | tf_op jit(solution)/shard_map/ppermute | solution.py:20
  17.0 2.8 %collective-permute-start.1 = (f32[512,256]{1,0:T(8,128)S(1)}, f32[512,256]{1,0:T(8,128)S(1)}, u32[]{:S(2)}, u32[]{:S(2)}) collective-permute-start(f32[512,256]{1,0:T(8,128)S(1)} %broadcast_select_fusion.3), channel_id=1, source_target_pairs={{0,192},{64,128},{128,64},{192,0},{1,193},{65,129},{129,65},{193,1... | collective-permute-start | bytes 1572872 | tf_op jit(solution)/shard_map/ppermute | solution.py:20
  21.6 2.4 %shard_map.69 = (bf16[4,2,256,512]{3,2,1,0:T(8,128)(2,1)S(1)}, bf16[4,2,256,512]{3,2,1,0:T(8,128)(2,1)S(1)}) custom-call(s32[4,256]{1,0:T(4,128)S(1)} %copy-done.1, f32[4,2,256,512]{3,2,1,0:T(8,128)S(1)} %copy-done), custom_call_target="tpu_custom_call" | custom-call | tf_op jit(solution)/shard_map/pallas_call | solution.py:106
  24.0 4.2 %collective-permute-done.2 = f32[512,256]{1,0:T(8,128)S(1)} collective-permute-done((f32[512,256]{1,0:T(8,128)S(1)}, f32[512,256]{1,0:T(8,128)S(1)}, u32[]{:S(2)}, u32[]{:S(2)}) %collective-permute-start.2) | collective-permute-done | bytes 524320 | tf_op jit(solution)/shard_map/ppermute | solution.py:20
  28.2 2.8 %collective-permute-start.4 = (f32[512,256]{1,0:T(8,128)S(1)}, f32[512,256]{1,0:T(8,128)S(1)}, u32[]{:S(2)}, u32[]{:S(2)}) collective-permute-start(f32[512,256]{1,0:T(8,128)S(1)} %broadcast_select_fusion.2), channel_id=1, source_target_pairs={{0,192},{64,128},{128,64},{192,0},{1,193},{65,129},{129,65},{193,1... | collective-permute-start | bytes 1572872 | tf_op jit(solution)/shard_map/ppermute | solution.py:20
  31.3 8.1 %collective-permute-done.5 = f32[512,256]{1,0:T(8,128)S(1)} collective-permute-done((f32[512,256]{1,0:T(8,128)S(1)}, f32[512,256]{1,0:T(8,128)S(1)}, u32[]{:S(2)}, u32[]{:S(2)}) %collective-permute-start.5) | collective-permute-done | bytes 524320 | tf_op jit(solution)/shard_map/ppermute | solution.py:20
  39.5 2.8 %collective-permute-start.8 = (f32[512,256]{1,0:T(8,128)S(1)}, f32[512,256]{1,0:T(8,128)S(1)}, u32[]{:S(2)}, u32[]{:S(2)}) collective-permute-start(f32[512,256]{1,0:T(8,128)S(1)} %broadcast_select_fusion.1), channel_id=1, source_target_pairs={{0,192},{64,128},{128,64},{192,0},{1,193},{65,129},{129,65},{193,1... | collective-permute-start | bytes 1572872 | tf_op jit(solution)/shard_map/ppermute | solution.py:20
  44.8 4.6 %collective-permute-done.9 = f32[512,256]{1,0:T(8,128)S(1)} collective-permute-done((f32[512,256]{1,0:T(8,128)S(1)}, f32[512,256]{1,0:T(8,128)S(1)}, u32[]{:S(2)}, u32[]{:S(2)}) %collective-permute-start.9) | collective-permute-done | bytes 524320 | tf_op jit(solution)/shard_map/ppermute | solution.py:20
  49.5 2.8 %collective-permute-start.14 = (f32[512,256]{1,0:T(8,128)S(1)}, f32[512,256]{1,0:T(8,128)S(1)}, u32[]{:S(2)}, u32[]{:S(2)}) collective-permute-start(f32[512,256]{1,0:T(8,128)S(1)} %broadcast_select_fusion), channel_id=1, source_target_pairs={{0,192},{64,128},{128,64},{192,0},{1,193},{65,129},{129,65},{193,1... | collective-permute-start | bytes 1572872 | tf_op jit(solution)/shard_map/ppermute | solution.py:20
  53.3 1.8 %collective-permute-start.12 = (f32[512,256]{1,0:T(8,128)S(1)}, f32[512,256]{1,0:T(8,128)S(1)}, u32[]{:S(2)}, u32[]{:S(2)}) collective-permute-start(f32[512,256]{1,0:T(8,128)S(1)} %shard_map.71.b.a), channel_id=1, source_target_pairs={{0,2},{1,3},{2,0},{3,1},{4,6},{5,7},{6,4},{7,5},{8,10},{9,11},{10,... | collective-permute-start | bytes 1572872 | tf_op jit(solution)/shard_map/ppermute | solution.py:20
  55.7 2.3 %collective-permute-done.6.b.a = f32[512,256]{1,0:T(8,128)S(1)} collective-permute-done((f32[512,256]{1,0:T(8,128)S(1)}, f32[512,256]{1,0:T(8,128)S(1)}, u32[]{:S(2)}, u32[]{:S(2)}) %collective-permute-start.6) | collective-permute-done | bytes 524320 | tf_op jit(solution)/shard_map/ppermute | solution.py:20
  58.6 3.1 %collective-permute-start.11 = (f32[512,256]{1,0:T(8,128)S(1)}, f32[512,256]{1,0:T(8,128)S(1)}, u32[]{:S(2)}, u32[]{:S(2)}) collective-permute-start(f32[512,256]{1,0:T(8,128)S(1)} %shard_map.74), channel_id=1, source_target_pairs={{0,6},{1,7},{2,4},{3,5},{4,2},{5,3},{6,0},{7,1},{8,14},{9,15},{10,... | collective-permute-start | bytes 1572872 | tf_op jit(solution)/shard_map/ppermute | solution.py:20
  61.7 1.9 %collective-permute-done.14 = f32[512,256]{1,0:T(8,128)S(1)} collective-permute-done((f32[512,256]{1,0:T(8,128)S(1)}, f32[512,256]{1,0:T(8,128)S(1)}, u32[]{:S(2)}, u32[]{:S(2)}) %collective-permute-start.14) | collective-permute-done | bytes 524320 | tf_op jit(solution)/shard_map/ppermute | solution.py:20
  66.2 3.0 %collective-permute-done.12.a.b = f32[512,256]{1,0:T(8,128)S(1)} collective-permute-done((f32[512,256]{1,0:T(8,128)S(1)}, f32[512,256]{1,0:T(8,128)S(1)}, u32[]{:S(2)}, u32[]{:S(2)}) %collective-permute-start.12) | collective-permute-done | bytes 524320 | tf_op jit(solution)/shard_map/ppermute | solution.py:20
  69.8 3.1 %collective-permute-start.16 = (f32[512,256]{1,0:T(8,128)S(1)}, f32[512,256]{1,0:T(8,128)S(1)}, u32[]{:S(2)}, u32[]{:S(2)}) collective-permute-start(f32[512,256]{1,0:T(8,128)S(1)} %shard_map.76), channel_id=1, source_target_pairs={{0,6},{1,7},{2,4},{3,5},{4,2},{5,3},{6,0},{7,1},{8,14},{9,15},{10,... | collective-permute-start | bytes 1572872 | tf_op jit(solution)/shard_map/ppermute | solution.py:20
  74.2 2.0 %collective-permute-start.15 = (f32[512,256]{1,0:T(8,128)S(1)}, f32[512,256]{1,0:T(8,128)S(1)}, u32[]{:S(2)}, u32[]{:S(2)}) collective-permute-start(f32[512,256]{1,0:T(8,128)S(1)} %shard_map.77.a), channel_id=1, source_target_pairs={{0,8},{1,9},{2,10},{3,11},{4,12},{5,13},{6,14},{7,15},{8,0},{9,1},... | collective-permute-start | bytes 1572872 | tf_op jit(solution)/shard_map/ppermute | solution.py:20
  77.7 2.8 %collective-permute-done.17.a.b = f32[512,256]{1,0:T(8,128)S(1)} collective-permute-done((f32[512,256]{1,0:T(8,128)S(1)}, f32[512,256]{1,0:T(8,128)S(1)}, u32[]{:S(2)}, u32[]{:S(2)}) %collective-permute-start.17) | collective-permute-done | bytes 524320 | tf_op jit(solution)/shard_map/ppermute | solution.py:20
  81.1 3.1 %collective-permute-start.21 = (f32[512,256]{1,0:T(8,128)S(1)}, f32[512,256]{1,0:T(8,128)S(1)}, u32[]{:S(2)}, u32[]{:S(2)}) collective-permute-start(f32[512,256]{1,0:T(8,128)S(1)} %shard_map.80), channel_id=1, source_target_pairs={{0,6},{1,7},{2,4},{3,5},{4,2},{5,3},{6,0},{7,1},{8,14},{9,15},{10,... | collective-permute-start | bytes 1572872 | tf_op jit(solution)/shard_map/ppermute | solution.py:20
  84.9 2.0 %collective-permute-start.20 = (f32[512,256]{1,0:T(8,128)S(1)}, f32[512,256]{1,0:T(8,128)S(1)}, u32[]{:S(2)}, u32[]{:S(2)}) collective-permute-start(f32[512,256]{1,0:T(8,128)S(1)} %shard_map.81.a), channel_id=1, source_target_pairs={{0,8},{1,9},{2,10},{3,11},{4,12},{5,13},{6,14},{7,15},{8,0},{9,1},... | collective-permute-start | bytes 1572872 | tf_op jit(solution)/shard_map/ppermute | solution.py:20
  89.5 1.8 %collective-permute-done.22.a.b = f32[512,256]{1,0:T(8,128)S(1)} collective-permute-done((f32[512,256]{1,0:T(8,128)S(1)}, f32[512,256]{1,0:T(8,128)S(1)}, u32[]{:S(2)}, u32[]{:S(2)}) %collective-permute-start.22) | collective-permute-done | bytes 524320 | tf_op jit(solution)/shard_map/ppermute | solution.py:20
  91.9 3.1 %collective-permute-start.26 = (f32[512,256]{1,0:T(8,128)S(1)}, f32[512,256]{1,0:T(8,128)S(1)}, u32[]{:S(2)}, u32[]{:S(2)}) collective-permute-start(f32[512,256]{1,0:T(8,128)S(1)} %shard_map.84), channel_id=1, source_target_pairs={{0,6},{1,7},{2,4},{3,5},{4,2},{5,3},{6,0},{7,1},{8,14},{9,15},{10,... | collective-permute-start | bytes 1572872 | tf_op jit(solution)/shard_map/ppermute | solution.py:20
  96.3 2.1 %collective-permute-start.25 = (f32[512,256]{1,0:T(8,128)S(1)}, f32[512,256]{1,0:T(8,128)S(1)}, u32[]{:S(2)}, u32[]{:S(2)}) collective-permute-start(f32[512,256]{1,0:T(8,128)S(1)} %shard_map.85.a), channel_id=1, source_target_pairs={{0,8},{1,9},{2,10},{3,11},{4,12},{5,13},{6,14},{7,15},{8,0},{9,1},... | collective-permute-start | bytes 1572872 | tf_op jit(solution)/shard_map/ppermute | solution.py:20
  102.2 4.6 %collective-permute-done.26.b = f32[512,256]{1,0:T(8,128)S(1)} collective-permute-done((f32[512,256]{1,0:T(8,128)S(1)}, f32[512,256]{1,0:T(8,128)S(1)}, u32[]{:S(2)}, u32[]{:S(2)}) %collective-permute-start.26) | collective-permute-done | bytes 524320 | tf_op jit(solution)/shard_map/ppermute | solution.py:20
  107.4 2.0 %collective-permute-start.29 = (f32[512,256]{1,0:T(8,128)S(1)}, f32[512,256]{1,0:T(8,128)S(1)}, u32[]{:S(2)}, u32[]{:S(2)}) collective-permute-start(f32[512,256]{1,0:T(8,128)S(1)} %shard_map.88.a), channel_id=1, source_target_pairs={{0,8},{1,9},{2,10},{3,11},{4,12},{5,13},{6,14},{7,15},{8,0},{9,1},... | collective-permute-start | bytes 1572872 | tf_op jit(solution)/shard_map/ppermute | solution.py:20
  113.5 7.5 %collective-permute-done.29.b = f32[512,256]{1,0:T(8,128)S(1)} collective-permute-done((f32[512,256]{1,0:T(8,128)S(1)}, f32[512,256]{1,0:T(8,128)S(1)}, u32[]{:S(2)}, u32[]{:S(2)}) %collective-permute-start.29) | collective-permute-done | bytes 524320 | tf_op jit(solution)/shard_map/ppermute | solution.py:20
  124.4 4.3 %collective-permute-done.31 = f32[256,256]{1,0:T(8,128)S(1)} collective-permute-done((f32[256,256]{1,0:T(8,128)S(1)}, f32[256,256]{1,0:T(8,128)S(1)}, u32[]{:S(2)}, u32[]{:S(2)}) %collective-permute-start.31) | collective-permute-done | bytes 262176 | tf_op jit(solution)/shard_map/ppermute | solution.py:20
  128.8 1.8 %collective-permute-start.32 = (f32[128,256]{1,0:T(8,128)S(1)}, f32[128,256]{1,0:T(8,128)S(1)}, u32[]{:S(2)}, u32[]{:S(2)}) collective-permute-start(f32[128,256]{1,0:T(8,128)S(1)} %slice_select_fusion.4), channel_id=1, source_target_pairs={{0,192},{64,128},{128,64},{192,0},{1,193},{65,129},{129,65},{193,1... | collective-permute-start | bytes 393224 | tf_op jit(solution)/shard_map/ppermute | solution.py:20
  131.2 3.8 %collective-permute-done.32 = f32[128,256]{1,0:T(8,128)S(1)} collective-permute-done((f32[128,256]{1,0:T(8,128)S(1)}, f32[128,256]{1,0:T(8,128)S(1)}, u32[]{:S(2)}, u32[]{:S(2)}) %collective-permute-start.32) | collective-permute-done | bytes 131104 | tf_op jit(solution)/shard_map/ppermute | solution.py:20
  (96 shorter events, 37.4 us)
Async XLA Ops:
  2.0 14.9 %collective-permute-start = (f32[512,256]{1,0:T(8,128)S(1)}, f32[512,256]{1,0:T(8,128)S(1)}, u32[]{:S(2)}, u32[]{:S(2)}) collective-permute-start(f32[512,256]{1,0:T(8,128)S(1)} %shard_map.65), channel_id=1, source_target_pairs={{0,64},{64,0},{128,192},{192,128},{1,65},{65,1},{129,193},{193,129... | collective-permute-start | bytes 1572872 | tf_op jit(solution)/shard_map/ppermute | solution.py:20
  5.6 22.5 %collective-permute-start.2 = (f32[512,256]{1,0:T(8,128)S(1)}, f32[512,256]{1,0:T(8,128)S(1)}, u32[]{:S(2)}, u32[]{:S(2)}) collective-permute-start(f32[512,256]{1,0:T(8,128)S(1)} %shard_map.66), channel_id=1, source_target_pairs={{0,64},{64,0},{128,192},{192,128},{1,65},{65,1},{129,193},{193,129... | collective-permute-start | bytes 1572872 | tf_op jit(solution)/shard_map/ppermute | solution.py:20
  8.3 31.1 %collective-permute-start.5 = (f32[512,256]{1,0:T(8,128)S(1)}, f32[512,256]{1,0:T(8,128)S(1)}, u32[]{:S(2)}, u32[]{:S(2)}) collective-permute-start(f32[512,256]{1,0:T(8,128)S(1)} %shard_map.67), channel_id=1, source_target_pairs={{0,64},{64,0},{128,192},{192,128},{1,65},{65,1},{129,193},{193,129... | collective-permute-start | bytes 1572872 | tf_op jit(solution)/shard_map/ppermute | solution.py:20
  11.9 37.6 %collective-permute-start.9 = (f32[512,256]{1,0:T(8,128)S(1)}, f32[512,256]{1,0:T(8,128)S(1)}, u32[]{:S(2)}, u32[]{:S(2)}) collective-permute-start(f32[512,256]{1,0:T(8,128)S(1)} %shard_map.68), channel_id=1, source_target_pairs={{0,64},{64,0},{128,192},{192,128},{1,65},{65,1},{129,193},{193,129... | collective-permute-start | bytes 1572872 | tf_op jit(solution)/shard_map/ppermute | solution.py:20
  17.0 14.1 %collective-permute-start.1 = (f32[512,256]{1,0:T(8,128)S(1)}, f32[512,256]{1,0:T(8,128)S(1)}, u32[]{:S(2)}, u32[]{:S(2)}) collective-permute-start(f32[512,256]{1,0:T(8,128)S(1)} %broadcast_select_fusion.3), channel_id=1, source_target_pairs={{0,192},{64,128},{128,64},{192,0},{1,193},{65,129},{129,65},{193,1... | collective-permute-start | bytes 1572872 | tf_op jit(solution)/shard_map/ppermute | solution.py:20
  19.9 35.2 %collective-permute-start.10 = (f32[2,256,512]{2,1,0:T(8,128)S(1)}, f32[2,256,512]{2,1,0:T(8,128)S(1)}, u32[]{:S(2)}, u32[]{:S(2)}) collective-permute-start(f32[2,256,512]{2,1,0:T(8,128)S(1)} %slice_bitcast_fusion), channel_id=1, source_target_pairs={{0,2},{1,3},{2,0},{3,1},{4,6},{5,7},{6,4},{7,5},{8,10},{9,11},{10,... | collective-permute-start | bytes 3145736 | tf_op jit(solution)/shard_map/ppermute | solution.py:20
  28.2 14.1 %collective-permute-start.4 = (f32[512,256]{1,0:T(8,128)S(1)}, f32[512,256]{1,0:T(8,128)S(1)}, u32[]{:S(2)}, u32[]{:S(2)}) collective-permute-start(f32[512,256]{1,0:T(8,128)S(1)} %broadcast_select_fusion.2), channel_id=1, source_target_pairs={{0,192},{64,128},{128,64},{192,0},{1,193},{65,129},{129,65},{193,1... | collective-permute-start | bytes 1572872 | tf_op jit(solution)/shard_map/ppermute | solution.py:20
  31.2 11.3 %collective-permute-start.3 = (f32[512,256]{1,0:T(8,128)S(1)}, f32[512,256]{1,0:T(8,128)S(1)}, u32[]{:S(2)}, u32[]{:S(2)}) collective-permute-start(f32[512,256]{1,0:T(8,128)S(1)} %select_select_fusion.3.a), channel_id=1, source_target_pairs={{0,1},{1,0},{2,3},{3,2},{4,5},{5,4},{6,7},{7,6},{8,9},{9,8},{10,11... | collective-permute-start | bytes 1572872 | tf_op jit(solution)/shard_map/ppermute | solution.py:20
  39.5 12.9 %collective-permute-start.8 = (f32[512,256]{1,0:T(8,128)S(1)}, f32[512,256]{1,0:T(8,128)S(1)}, u32[]{:S(2)}, u32[]{:S(2)}) collective-permute-start(f32[512,256]{1,0:T(8,128)S(1)} %broadcast_select_fusion.1), channel_id=1, source_target_pairs={{0,192},{64,128},{128,64},{192,0},{1,193},{65,129},{129,65},{193,1... | collective-permute-start | bytes 1572872 | tf_op jit(solution)/shard_map/ppermute | solution.py:20
  42.4 10.2 %collective-permute-start.7 = (f32[512,256]{1,0:T(8,128)S(1)}, f32[512,256]{1,0:T(8,128)S(1)}, u32[]{:S(2)}, u32[]{:S(2)}) collective-permute-start(f32[512,256]{1,0:T(8,128)S(1)} %select_select_fusion.2.a), channel_id=1, source_target_pairs={{0,1},{1,0},{2,3},{3,2},{4,5},{5,4},{6,7},{7,6},{8,9},{9,8},{10,11... | collective-permute-start | bytes 1572872 | tf_op jit(solution)/shard_map/ppermute | solution.py:20
  43.2 14.8 %collective-permute-start.6 = (f32[512,256]{1,0:T(8,128)S(1)}, f32[512,256]{1,0:T(8,128)S(1)}, u32[]{:S(2)}, u32[]{:S(2)}) collective-permute-start(f32[512,256]{1,0:T(8,128)S(1)} %shard_map.70.a.b), channel_id=1, source_target_pairs={{0,2},{1,3},{2,0},{3,1},{4,6},{5,7},{6,4},{7,5},{8,10},{9,11},{10,... | collective-permute-start | bytes 1572872 | tf_op jit(solution)/shard_map/ppermute | solution.py:20
  49.5 14.1 %collective-permute-start.14 = (f32[512,256]{1,0:T(8,128)S(1)}, f32[512,256]{1,0:T(8,128)S(1)}, u32[]{:S(2)}, u32[]{:S(2)}) collective-permute-start(f32[512,256]{1,0:T(8,128)S(1)} %broadcast_select_fusion), channel_id=1, source_target_pairs={{0,192},{64,128},{128,64},{192,0},{1,193},{65,129},{129,65},{193,1... | collective-permute-start | bytes 1572872 | tf_op jit(solution)/shard_map/ppermute | solution.py:20
  52.5 11.3 %collective-permute-start.13 = (f32[512,256]{1,0:T(8,128)S(1)}, f32[512,256]{1,0:T(8,128)S(1)}, u32[]{:S(2)}, u32[]{:S(2)}) collective-permute-start(f32[512,256]{1,0:T(8,128)S(1)} %select_select_fusion.1.a), channel_id=1, source_target_pairs={{0,1},{1,0},{2,3},{3,2},{4,5},{5,4},{6,7},{7,6},{8,9},{9,8},{10,11... | collective-permute-start | bytes 1572872 | tf_op jit(solution)/shard_map/ppermute | solution.py:20
  53.3 15.9 %collective-permute-start.12 = (f32[512,256]{1,0:T(8,128)S(1)}, f32[512,256]{1,0:T(8,128)S(1)}, u32[]{:S(2)}, u32[]{:S(2)}) collective-permute-start(f32[512,256]{1,0:T(8,128)S(1)} %shard_map.71.b.a), channel_id=1, source_target_pairs={{0,2},{1,3},{2,0},{3,1},{4,6},{5,7},{6,4},{7,5},{8,10},{9,11},{10,... | collective-permute-start | bytes 1572872 | tf_op jit(solution)/shard_map/ppermute | solution.py:20
  58.6 15.0 %collective-permute-start.11 = (f32[512,256]{1,0:T(8,128)S(1)}, f32[512,256]{1,0:T(8,128)S(1)}, u32[]{:S(2)}, u32[]{:S(2)}) collective-permute-start(f32[512,256]{1,0:T(8,128)S(1)} %shard_map.74), channel_id=1, source_target_pairs={{0,6},{1,7},{2,4},{3,5},{4,2},{5,3},{6,0},{7,1},{8,14},{9,15},{10,... | collective-permute-start | bytes 1572872 | tf_op jit(solution)/shard_map/ppermute | solution.py:20
  63.8 13.1 %collective-permute-start.18 = (f32[512,256]{1,0:T(8,128)S(1)}, f32[512,256]{1,0:T(8,128)S(1)}, u32[]{:S(2)}, u32[]{:S(2)}) collective-permute-start(f32[512,256]{1,0:T(8,128)S(1)} %select_select_fusion.a), channel_id=1, source_target_pairs={{0,1},{1,0},{2,3},{3,2},{4,5},{5,4},{6,7},{7,6},{8,9},{9,8},{10,11... | collective-permute-start | bytes 1572872 | tf_op jit(solution)/shard_map/ppermute | solution.py:20
  64.5 16.0 %collective-permute-start.17 = (f32[512,256]{1,0:T(8,128)S(1)}, f32[512,256]{1,0:T(8,128)S(1)}, u32[]{:S(2)}, u32[]{:S(2)}) collective-permute-start(f32[512,256]{1,0:T(8,128)S(1)} %shard_map.75.b.a), channel_id=1, source_target_pairs={{0,2},{1,3},{2,0},{3,1},{4,6},{5,7},{6,4},{7,5},{8,10},{9,11},{10,... | collective-permute-start | bytes 1572872 | tf_op jit(solution)/shard_map/ppermute | solution.py:20
  69.8 14.5 %collective-permute-start.16 = (f32[512,256]{1,0:T(8,128)S(1)}, f32[512,256]{1,0:T(8,128)S(1)}, u32[]{:S(2)}, u32[]{:S(2)}) collective-permute-start(f32[512,256]{1,0:T(8,128)S(1)} %shard_map.76), channel_id=1, source_target_pairs={{0,6},{1,7},{2,4},{3,5},{4,2},{5,3},{6,0},{7,1},{8,14},{9,15},{10,... | collective-permute-start | bytes 1572872 | tf_op jit(solution)/shard_map/ppermute | solution.py:20
  74.2 13.7 %collective-permute-start.15 = (f32[512,256]{1,0:T(8,128)S(1)}, f32[512,256]{1,0:T(8,128)S(1)}, u32[]{:S(2)}, u32[]{:S(2)}) collective-permute-start(f32[512,256]{1,0:T(8,128)S(1)} %shard_map.77.a), channel_id=1, source_target_pairs={{0,8},{1,9},{2,10},{3,11},{4,12},{5,13},{6,14},{7,15},{8,0},{9,1},... | collective-permute-start | bytes 1572872 | tf_op jit(solution)/shard_map/ppermute | solution.py:20
  77.5 13.8 %collective-permute-start.22 = (f32[512,256]{1,0:T(8,128)S(1)}, f32[512,256]{1,0:T(8,128)S(1)}, u32[]{:S(2)}, u32[]{:S(2)}) collective-permute-start(f32[512,256]{1,0:T(8,128)S(1)} %shard_map.79.b.a), channel_id=1, source_target_pairs={{0,2},{1,3},{2,0},{3,1},{4,6},{5,7},{6,4},{7,5},{8,10},{9,11},{10,... | collective-permute-start | bytes 1572872 | tf_op jit(solution)/shard_map/ppermute | solution.py:20
  81.1 14.6 %collective-permute-start.21 = (f32[512,256]{1,0:T(8,128)S(1)}, f32[512,256]{1,0:T(8,128)S(1)}, u32[]{:S(2)}, u32[]{:S(2)}) collective-permute-start(f32[512,256]{1,0:T(8,128)S(1)} %shard_map.80), channel_id=1, source_target_pairs={{0,6},{1,7},{2,4},{3,5},{4,2},{5,3},{6,0},{7,1},{8,14},{9,15},{10,... | collective-permute-start | bytes 1572872 | tf_op jit(solution)/shard_map/ppermute | solution.py:20
  84.9 13.9 %collective-permute-start.20 = (f32[512,256]{1,0:T(8,128)S(1)}, f32[512,256]{1,0:T(8,128)S(1)}, u32[]{:S(2)}, u32[]{:S(2)}) collective-permute-start(f32[512,256]{1,0:T(8,128)S(1)} %shard_map.81.a), channel_id=1, source_target_pairs={{0,8},{1,9},{2,10},{3,11},{4,12},{5,13},{6,14},{7,15},{8,0},{9,1},... | collective-permute-start | bytes 1572872 | tf_op jit(solution)/shard_map/ppermute | solution.py:20
  88.5 12.0 %collective-permute-start.19 = (f32[256,256]{1,0:T(8,128)S(1)}, f32[256,256]{1,0:T(8,128)S(1)}, u32[]{:S(2)}, u32[]{:S(2)}) collective-permute-start(f32[256,256]{1,0:T(8,128)S(1)} %slice_select_fusion.3), channel_id=1, source_target_pairs={{0,64},{64,0},{128,192},{192,128},{1,65},{65,1},{129,193},{193,129... | collective-permute-start | bytes 786440 | tf_op jit(solution)/shard_map/ppermute | solution.py:20
  91.9 14.9 %collective-permute-start.26 = (f32[512,256]{1,0:T(8,128)S(1)}, f32[512,256]{1,0:T(8,128)S(1)}, u32[]{:S(2)}, u32[]{:S(2)}) collective-permute-start(f32[512,256]{1,0:T(8,128)S(1)} %shard_map.84), channel_id=1, source_target_pairs={{0,6},{1,7},{2,4},{3,5},{4,2},{5,3},{6,0},{7,1},{8,14},{9,15},{10,... | collective-permute-start | bytes 1572872 | tf_op jit(solution)/shard_map/ppermute | solution.py:20
  96.3 14.0 %collective-permute-start.25 = (f32[512,256]{1,0:T(8,128)S(1)}, f32[512,256]{1,0:T(8,128)S(1)}, u32[]{:S(2)}, u32[]{:S(2)}) collective-permute-start(f32[512,256]{1,0:T(8,128)S(1)} %shard_map.85.a), channel_id=1, source_target_pairs={{0,8},{1,9},{2,10},{3,11},{4,12},{5,13},{6,14},{7,15},{8,0},{9,1},... | collective-permute-start | bytes 1572872 | tf_op jit(solution)/shard_map/ppermute | solution.py:20
  100.2 11.1 %collective-permute-start.24 = (f32[256,256]{1,0:T(8,128)S(1)}, f32[256,256]{1,0:T(8,128)S(1)}, u32[]{:S(2)}, u32[]{:S(2)}) collective-permute-start(f32[256,256]{1,0:T(8,128)S(1)} %slice_select_fusion.2), channel_id=1, source_target_pairs={{0,64},{64,0},{128,192},{192,128},{1,65},{65,1},{129,193},{193,129... | collective-permute-start | bytes 786440 | tf_op jit(solution)/shard_map/ppermute | solution.py:20
  100.6 12.3 %collective-permute-start.23 = (f32[128,256]{1,0:T(8,128)S(1)}, f32[128,256]{1,0:T(8,128)S(1)}, u32[]{:S(2)}, u32[]{:S(2)}) collective-permute-start(f32[128,256]{1,0:T(8,128)S(1)} %slice_select_fusion.7), channel_id=1, source_target_pairs={{0,192},{64,128},{128,64},{192,0},{1,193},{65,129},{129,65},{193,1... | collective-permute-start | bytes 393224 | tf_op jit(solution)/shard_map/ppermute | solution.py:20
  107.4 13.6 %collective-permute-start.29 = (f32[512,256]{1,0:T(8,128)S(1)}, f32[512,256]{1,0:T(8,128)S(1)}, u32[]{:S(2)}, u32[]{:S(2)}) collective-permute-start(f32[512,256]{1,0:T(8,128)S(1)} %shard_map.88.a), channel_id=1, source_target_pairs={{0,8},{1,9},{2,10},{3,11},{4,12},{5,13},{6,14},{7,15},{8,0},{9,1},... | collective-permute-start | bytes 1572872 | tf_op jit(solution)/shard_map/ppermute | solution.py:20
  111.0 11.0 %collective-permute-start.28 = (f32[256,256]{1,0:T(8,128)S(1)}, f32[256,256]{1,0:T(8,128)S(1)}, u32[]{:S(2)}, u32[]{:S(2)}) collective-permute-start(f32[256,256]{1,0:T(8,128)S(1)} %slice_select_fusion.1), channel_id=1, source_target_pairs={{0,64},{64,0},{128,192},{192,128},{1,65},{65,1},{129,193},{193,129... | collective-permute-start | bytes 786440 | tf_op jit(solution)/shard_map/ppermute | solution.py:20
  111.4 12.4 %collective-permute-start.27 = (f32[128,256]{1,0:T(8,128)S(1)}, f32[128,256]{1,0:T(8,128)S(1)}, u32[]{:S(2)}, u32[]{:S(2)}) collective-permute-start(f32[128,256]{1,0:T(8,128)S(1)} %slice_select_fusion.6), channel_id=1, source_target_pairs={{0,192},{64,128},{128,64},{192,0},{1,193},{65,129},{129,65},{193,1... | collective-permute-start | bytes 393224 | tf_op jit(solution)/shard_map/ppermute | solution.py:20
  121.7 7.0 %collective-permute-start.31 = (f32[256,256]{1,0:T(8,128)S(1)}, f32[256,256]{1,0:T(8,128)S(1)}, u32[]{:S(2)}, u32[]{:S(2)}) collective-permute-start(f32[256,256]{1,0:T(8,128)S(1)} %slice_select_fusion), channel_id=1, source_target_pairs={{0,64},{64,0},{128,192},{192,128},{1,65},{65,1},{129,193},{193,129... | collective-permute-start | bytes 786440 | tf_op jit(solution)/shard_map/ppermute | solution.py:20
  122.1 8.5 %collective-permute-start.30 = (f32[128,256]{1,0:T(8,128)S(1)}, f32[128,256]{1,0:T(8,128)S(1)}, u32[]{:S(2)}, u32[]{:S(2)}) collective-permute-start(f32[128,256]{1,0:T(8,128)S(1)} %slice_select_fusion.5), channel_id=1, source_target_pairs={{0,192},{64,128},{128,64},{192,0},{1,193},{65,129},{129,65},{193,1... | collective-permute-start | bytes 393224 | tf_op jit(solution)/shard_map/ppermute | solution.py:20
  (5 other events, 41.1 us)

commit v4 on v3

--- a/solution.py
+++ b/solution.py
@@ -134,6 +134,31 @@
         compiler_params=pltpu.CompilerParams(vmem_limit_bytes=LIMIT),
         cost_estimate=CHEAP,
     )(a, b, *mats)
+
+
+def expand_kernel(src, *refs):
+    *blocks, out = refs
+    n = pl.program_id(0) * 2 + pl.program_id(1)
+    for k, block in enumerate(blocks):
+
+        @pl.when(n == k)
+        def _():
+            out[...] = dot3(halves(block[...]), halves(src[0]), NT)
+
+
+def expand(blocks, src_basis):
+    nodes, leaf, rank = src_basis.shape
+    width = blocks[0].shape[0]
+    return pl.pallas_call(
+        expand_kernel,
+        grid=(nodes, 2),
+        in_specs=[pl.BlockSpec((1, leaf, rank), lambda j, h: (j, 0, 0))]
+        + [pl.BlockSpec(block.shape, lambda j, h: (0, 0)) for block in blocks],
+        out_specs=pl.BlockSpec((width, leaf), lambda j, h: (h, j)),
+        out_shape=jax.ShapeDtypeStruct((2 * width, nodes * leaf), jnp.float32),
+        compiler_params=pltpu.CompilerParams(vmem_limit_bytes=LIMIT),
+        cost_estimate=CHEAP,
+    )(src_basis, *blocks)
 
 
 def body(obs_field, observer_leaf_bases, transfer, src_basis, leaf_map, partner_perm):
@@ -172,11 +197,7 @@
         sent = where(4, end, top)
         got = yield sent, flipped(sent, "obs", 3)
         c = where(4, top, end) + got
-        out = lax.dot_general(
-            c, src_basis[j], NT, precision=lax.Precision.HIGHEST,
-            preferred_element_type=jnp.float32,
-        )
-        yield out, out
+        yield c, c
 
     chains = {}
     waiting = {}
@@ -191,16 +212,7 @@
         else:
             value, _ = lax.optimization_barrier((waiting[n], last))
             last, waiting[n] = chains[n].send(value)
-    rows = {}
-    for n, (node, at, width) in enumerate(CHUNKS):
-        rows.setdefault(node, {})[at] = waiting[n]
-    return jnp.concatenate(
-        [
-            jnp.concatenate([rows[node][at] for at in sorted(rows[node])], 0)
-            for node in range(nodes)
-        ],
-        1,
-    )
+    return expand([waiting[n] for n in range(len(CHUNKS))], src_basis)
 
 
 def solution(mesh):

time: 137 us -> 138 us (level)
  Pallas kernels: 23.5 us -> 26.2 us
  matrix products: 2.51 us -> 0 us
  waiting for transfers between devices: 56.1 us -> 58.1 us
    pallas_call x0 -> x1, Pallas kernels: none -> 2.67 us  [expand(): pl.pallas_call(expand_kernel, grid=(nodes, 2), in_specs=[pl.BlockSpec((1,...]
    dot_general x4 -> x0, matrix products: 2.51 us -> none  [chain(): lax.dot_general(c, src_basis[j], NT, precision=lax.Precision.HIGHEST, pre...]
    ppermute x33, waiting for transfers between devices: 56.1 us -> 58.1 us  [flipped(): return lax.ppermute(block, axis, [(i, i ^ mask) for i in range(count)])]
  transfers between devices with their start and end apart: 33 -> 33, of which waited for: 18 -> 18; matrix products, arithmetic and copies ran while one was open for 2% -> 1% of each run, Pallas kernels for 16% -> 16%
where the time goes in v4:
time: 138 us
  waiting for transfers between devices  58.1 us (42%)
  starting transfers between devices  51.7 us (37%)
  Pallas kernels  26.2 us (19%)
    ppermute x33, waiting for transfers between devices, flipped(): return lax.ppermute(block, axis, [(i, i ^ mask) for i in range(count)])  58.1 us
    ppermute x33, starting transfers between devices, flipped(): return lax.ppermute(block, axis, [(i, i ^ mask) for i in range(count)])  51.7 us
    pallas_call x20, Pallas kernels, step(): pl.pallas_call(step_kernel, grid=(1,), in_specs=[whole, whole, one, one],...  12.4 us
    pallas_call x4, Pallas kernels, project(): pl.pallas_call(project_kernel, grid=(1,), in_specs=columns + [pl.BlockSpe...  8.05 us
    pallas_call x2, Pallas kernels, prepare(): pl.pallas_call(functools.partial(prepare_kernel, first), grid=(levels, no...  3.01 us
  transfers between devices with their start and end apart: 33, of which 18 were waited for; matrix products, arithmetic and copies ran while one was open for 1% of the time, Pallas kernels for 16%

profile of v4, /device:TPU:64, one launch (start us, length us, event | category | flops | bytes accessed | tf_op | source)
XLA Modules:
  0.0 137.8 jit_solution(700646142736595089)
XLA Ops:
  0.0 2.0 %shard_map.65 = f32[512,256]{1,0:T(8,128)S(1)} custom-call(f32[1024,1024]{1,0:T(8,128)} %refs_3_.7, f32[1024,1024]{1,0:T(8,128)} %refs_3_.7, f32[1024,1024]{1,0:T(8,128)} %refs_3_.7, f32[1024,1024]{1,0:T(8,128)} %refs_3_.7, f32[2,512,256]{2,1,0:T(8,128)} %refs_4_.4), custom_call_target="tpu_custom_call" | custom-call | tf_op jit(solution)/shard_map/pallas_call | solution.py:80
  3.6 2.0 %shard_map.66 = f32[512,256]{1,0:T(8,128)S(1)} custom-call(f32[1024,1024]{1,0:T(8,128)} %refs_3_.7, f32[1024,1024]{1,0:T(8,128)} %refs_3_.7, f32[1024,1024]{1,0:T(8,128)} %refs_3_.7, f32[1024,1024]{1,0:T(8,128)} %refs_3_.7, f32[2,512,256]{2,1,0:T(8,128)} %refs_4_.4), custom_call_target="tpu_custom_call" | custom-call | tf_op jit(solution)/shard_map/pallas_call | solution.py:80
  6.2 2.0 %shard_map.67 = f32[512,256]{1,0:T(8,128)S(1)} custom-call(f32[1024,1024]{1,0:T(8,128)} %refs_3_.7, f32[1024,1024]{1,0:T(8,128)} %refs_3_.7, f32[1024,1024]{1,0:T(8,128)} %refs_3_.7, f32[1024,1024]{1,0:T(8,128)} %refs_3_.7, f32[2,512,256]{2,1,0:T(8,128)} %refs_4_.4), custom_call_target="tpu_custom_call" | custom-call | tf_op jit(solution)/shard_map/pallas_call | solution.py:80
  9.9 2.0 %shard_map.68 = f32[512,256]{1,0:T(8,128)S(1)} custom-call(f32[1024,1024]{1,0:T(8,128)} %refs_3_.7, f32[1024,1024]{1,0:T(8,128)} %refs_3_.7, f32[1024,1024]{1,0:T(8,128)} %refs_3_.7, f32[1024,1024]{1,0:T(8,128)} %refs_3_.7, f32[2,512,256]{2,1,0:T(8,128)} %refs_4_.4), custom_call_target="tpu_custom_call" | custom-call | tf_op jit(solution)/shard_map/pallas_call | solution.py:80
  13.0 3.9 %collective-permute-done = f32[512,256]{1,0:T(8,128)S(1)} collective-permute-done((f32[512,256]{1,0:T(8,128)S(1)}, f32[512,256]{1,0:T(8,128)S(1)}, u32[]{:S(2)}, u32[]{:S(2)}) %collective-permute-start) | collective-permute-done | bytes 524320 | tf_op jit(solution)/shard_map/ppermute | solution.py:20
  17.0 2.8 %collective-permute-start.1 = (f32[512,256]{1,0:T(8,128)S(1)}, f32[512,256]{1,0:T(8,128)S(1)}, u32[]{:S(2)}, u32[]{:S(2)}) collective-permute-start(f32[512,256]{1,0:T(8,128)S(1)} %broadcast_select_fusion.3), channel_id=1, source_target_pairs={{0,192},{64,128},{128,64},{192,0},{1,193},{65,129},{129,65},{193,1... | collective-permute-start | bytes 1572872 | tf_op jit(solution)/shard_map/ppermute | solution.py:20
  21.6 2.4 %shard_map.69 = (bf16[4,2,256,512]{3,2,1,0:T(8,128)(2,1)S(1)}, bf16[4,2,256,512]{3,2,1,0:T(8,128)(2,1)S(1)}) custom-call(s32[4,256]{1,0:T(4,128)S(1)} %copy-done.2, f32[4,2,256,512]{3,2,1,0:T(8,128)S(1)} %copy-done), custom_call_target="tpu_custom_call" | custom-call | tf_op jit(solution)/shard_map/pallas_call | solution.py:106
  24.0 4.2 %collective-permute-done.2 = f32[512,256]{1,0:T(8,128)S(1)} collective-permute-done((f32[512,256]{1,0:T(8,128)S(1)}, f32[512,256]{1,0:T(8,128)S(1)}, u32[]{:S(2)}, u32[]{:S(2)}) %collective-permute-start.2) | collective-permute-done | bytes 524320 | tf_op jit(solution)/shard_map/ppermute | solution.py:20
  28.2 2.8 %collective-permute-start.4 = (f32[512,256]{1,0:T(8,128)S(1)}, f32[512,256]{1,0:T(8,128)S(1)}, u32[]{:S(2)}, u32[]{:S(2)}) collective-permute-start(f32[512,256]{1,0:T(8,128)S(1)} %broadcast_select_fusion.2), channel_id=1, source_target_pairs={{0,192},{64,128},{128,64},{192,0},{1,193},{65,129},{129,65},{193,1... | collective-permute-start | bytes 1572872 | tf_op jit(solution)/shard_map/ppermute | solution.py:20
  31.3 8.1 %collective-permute-done.5 = f32[512,256]{1,0:T(8,128)S(1)} collective-permute-done((f32[512,256]{1,0:T(8,128)S(1)}, f32[512,256]{1,0:T(8,128)S(1)}, u32[]{:S(2)}, u32[]{:S(2)}) %collective-permute-start.5) | collective-permute-done | bytes 524320 | tf_op jit(solution)/shard_map/ppermute | solution.py:20
  39.5 2.8 %collective-permute-start.8 = (f32[512,256]{1,0:T(8,128)S(1)}, f32[512,256]{1,0:T(8,128)S(1)}, u32[]{:S(2)}, u32[]{:S(2)}) collective-permute-start(f32[512,256]{1,0:T(8,128)S(1)} %broadcast_select_fusion.1), channel_id=1, source_target_pairs={{0,192},{64,128},{128,64},{192,0},{1,193},{65,129},{129,65},{193,1... | collective-permute-start | bytes 1572872 | tf_op jit(solution)/shard_map/ppermute | solution.py:20
  44.8 4.7 %collective-permute-done.9 = f32[512,256]{1,0:T(8,128)S(1)} collective-permute-done((f32[512,256]{1,0:T(8,128)S(1)}, f32[512,256]{1,0:T(8,128)S(1)}, u32[]{:S(2)}, u32[]{:S(2)}) %collective-permute-start.9) | collective-permute-done | bytes 524320 | tf_op jit(solution)/shard_map/ppermute | solution.py:20
  49.5 2.8 %collective-permute-start.14 = (f32[512,256]{1,0:T(8,128)S(1)}, f32[512,256]{1,0:T(8,128)S(1)}, u32[]{:S(2)}, u32[]{:S(2)}) collective-permute-start(f32[512,256]{1,0:T(8,128)S(1)} %broadcast_select_fusion), channel_id=1, source_target_pairs={{0,192},{64,128},{128,64},{192,0},{1,193},{65,129},{129,65},{193,1... | collective-permute-start | bytes 1572872 | tf_op jit(solution)/shard_map/ppermute | solution.py:20
  53.3 1.8 %collective-permute-start.12 = (f32[512,256]{1,0:T(8,128)S(1)}, f32[512,256]{1,0:T(8,128)S(1)}, u32[]{:S(2)}, u32[]{:S(2)}) collective-permute-start(f32[512,256]{1,0:T(8,128)S(1)} %shard_map.71.b.a), channel_id=1, source_target_pairs={{0,2},{1,3},{2,0},{3,1},{4,6},{5,7},{6,4},{7,5},{8,10},{9,11},{10,... | collective-permute-start | bytes 1572872 | tf_op jit(solution)/shard_map/ppermute | solution.py:20
  55.7 2.2 %collective-permute-done.6.b.a = f32[512,256]{1,0:T(8,128)S(1)} collective-permute-done((f32[512,256]{1,0:T(8,128)S(1)}, f32[512,256]{1,0:T(8,128)S(1)}, u32[]{:S(2)}, u32[]{:S(2)}) %collective-permute-start.6) | collective-permute-done | bytes 524320 | tf_op jit(solution)/shard_map/ppermute | solution.py:20
  58.6 3.1 %collective-permute-start.11 = (f32[512,256]{1,0:T(8,128)S(1)}, f32[512,256]{1,0:T(8,128)S(1)}, u32[]{:S(2)}, u32[]{:S(2)}) collective-permute-start(f32[512,256]{1,0:T(8,128)S(1)} %shard_map.74), channel_id=1, source_target_pairs={{0,6},{1,7},{2,4},{3,5},{4,2},{5,3},{6,0},{7,1},{8,14},{9,15},{10,... | collective-permute-start | bytes 1572872 | tf_op jit(solution)/shard_map/ppermute | solution.py:20
  61.7 1.9 %collective-permute-done.14 = f32[512,256]{1,0:T(8,128)S(1)} collective-permute-done((f32[512,256]{1,0:T(8,128)S(1)}, f32[512,256]{1,0:T(8,128)S(1)}, u32[]{:S(2)}, u32[]{:S(2)}) %collective-permute-start.14) | collective-permute-done | bytes 524320 | tf_op jit(solution)/shard_map/ppermute | solution.py:20
  66.2 3.1 %collective-permute-done.12.a.b = f32[512,256]{1,0:T(8,128)S(1)} collective-permute-done((f32[512,256]{1,0:T(8,128)S(1)}, f32[512,256]{1,0:T(8,128)S(1)}, u32[]{:S(2)}, u32[]{:S(2)}) %collective-permute-start.12) | collective-permute-done | bytes 524320 | tf_op jit(solution)/shard_map/ppermute | solution.py:20
  69.8 3.1 %collective-permute-start.16 = (f32[512,256]{1,0:T(8,128)S(1)}, f32[512,256]{1,0:T(8,128)S(1)}, u32[]{:S(2)}, u32[]{:S(2)}) collective-permute-start(f32[512,256]{1,0:T(8,128)S(1)} %shard_map.76), channel_id=1, source_target_pairs={{0,6},{1,7},{2,4},{3,5},{4,2},{5,3},{6,0},{7,1},{8,14},{9,15},{10,... | collective-permute-start | bytes 1572872 | tf_op jit(solution)/shard_map/ppermute | solution.py:20
  74.2 2.0 %collective-permute-start.15 = (f32[512,256]{1,0:T(8,128)S(1)}, f32[512,256]{1,0:T(8,128)S(1)}, u32[]{:S(2)}, u32[]{:S(2)}) collective-permute-start(f32[512,256]{1,0:T(8,128)S(1)} %shard_map.77.a), channel_id=1, source_target_pairs={{0,8},{1,9},{2,10},{3,11},{4,12},{5,13},{6,14},{7,15},{8,0},{9,1},... | collective-permute-start | bytes 1572872 | tf_op jit(solution)/shard_map/ppermute | solution.py:20
  77.7 2.8 %collective-permute-done.17.a.b = f32[512,256]{1,0:T(8,128)S(1)} collective-permute-done((f32[512,256]{1,0:T(8,128)S(1)}, f32[512,256]{1,0:T(8,128)S(1)}, u32[]{:S(2)}, u32[]{:S(2)}) %collective-permute-start.17) | collective-permute-done | bytes 524320 | tf_op jit(solution)/shard_map/ppermute | solution.py:20
  81.1 3.1 %collective-permute-start.21 = (f32[512,256]{1,0:T(8,128)S(1)}, f32[512,256]{1,0:T(8,128)S(1)}, u32[]{:S(2)}, u32[]{:S(2)}) collective-permute-start(f32[512,256]{1,0:T(8,128)S(1)} %shard_map.80), channel_id=1, source_target_pairs={{0,6},{1,7},{2,4},{3,5},{4,2},{5,3},{6,0},{7,1},{8,14},{9,15},{10,... | collective-permute-start | bytes 1572872 | tf_op jit(solution)/shard_map/ppermute | solution.py:20
  85.0 2.0 %collective-permute-start.20 = (f32[512,256]{1,0:T(8,128)S(1)}, f32[512,256]{1,0:T(8,128)S(1)}, u32[]{:S(2)}, u32[]{:S(2)}) collective-permute-start(f32[512,256]{1,0:T(8,128)S(1)} %shard_map.81.a), channel_id=1, source_target_pairs={{0,8},{1,9},{2,10},{3,11},{4,12},{5,13},{6,14},{7,15},{8,0},{9,1},... | collective-permute-start | bytes 1572872 | tf_op jit(solution)/shard_map/ppermute | solution.py:20
  89.5 1.8 %collective-permute-done.22.a.b = f32[512,256]{1,0:T(8,128)S(1)} collective-permute-done((f32[512,256]{1,0:T(8,128)S(1)}, f32[512,256]{1,0:T(8,128)S(1)}, u32[]{:S(2)}, u32[]{:S(2)}) %collective-permute-start.22) | collective-permute-done | bytes 524320 | tf_op jit(solution)/shard_map/ppermute | solution.py:20
  91.9 3.1 %collective-permute-start.26 = (f32[512,256]{1,0:T(8,128)S(1)}, f32[512,256]{1,0:T(8,128)S(1)}, u32[]{:S(2)}, u32[]{:S(2)}) collective-permute-start(f32[512,256]{1,0:T(8,128)S(1)} %shard_map.84), channel_id=1, source_target_pairs={{0,6},{1,7},{2,4},{3,5},{4,2},{5,3},{6,0},{7,1},{8,14},{9,15},{10,... | collective-permute-start | bytes 1572872 | tf_op jit(solution)/shard_map/ppermute | solution.py:20
  96.3 2.1 %collective-permute-start.25 = (f32[512,256]{1,0:T(8,128)S(1)}, f32[512,256]{1,0:T(8,128)S(1)}, u32[]{:S(2)}, u32[]{:S(2)}) collective-permute-start(f32[512,256]{1,0:T(8,128)S(1)} %shard_map.85.a), channel_id=1, source_target_pairs={{0,8},{1,9},{2,10},{3,11},{4,12},{5,13},{6,14},{7,15},{8,0},{9,1},... | collective-permute-start | bytes 1572872 | tf_op jit(solution)/shard_map/ppermute | solution.py:20
  102.1 4.6 %collective-permute-done.26.b = f32[512,256]{1,0:T(8,128)S(1)} collective-permute-done((f32[512,256]{1,0:T(8,128)S(1)}, f32[512,256]{1,0:T(8,128)S(1)}, u32[]{:S(2)}, u32[]{:S(2)}) %collective-permute-start.26) | collective-permute-done | bytes 524320 | tf_op jit(solution)/shard_map/ppermute | solution.py:20
  107.4 2.0 %collective-permute-start.29 = (f32[512,256]{1,0:T(8,128)S(1)}, f32[512,256]{1,0:T(8,128)S(1)}, u32[]{:S(2)}, u32[]{:S(2)}) collective-permute-start(f32[512,256]{1,0:T(8,128)S(1)} %shard_map.88.a), channel_id=1, source_target_pairs={{0,8},{1,9},{2,10},{3,11},{4,12},{5,13},{6,14},{7,15},{8,0},{9,1},... | collective-permute-start | bytes 1572872 | tf_op jit(solution)/shard_map/ppermute | solution.py:20
  112.8 8.2 %collective-permute-done.29.b = f32[512,256]{1,0:T(8,128)S(1)} collective-permute-done((f32[512,256]{1,0:T(8,128)S(1)}, f32[512,256]{1,0:T(8,128)S(1)}, u32[]{:S(2)}, u32[]{:S(2)}) %collective-permute-start.29) | collective-permute-done | bytes 524320 | tf_op jit(solution)/shard_map/ppermute | solution.py:20
  123.8 4.9 %collective-permute-done.31 = f32[256,256]{1,0:T(8,128)S(1)} collective-permute-done((f32[256,256]{1,0:T(8,128)S(1)}, f32[256,256]{1,0:T(8,128)S(1)}, u32[]{:S(2)}, u32[]{:S(2)}) %collective-permute-start.31) | collective-permute-done | bytes 262176 | tf_op jit(solution)/shard_map/ppermute | solution.py:20
  130.6 4.5 %collective-permute-done.32 = f32[128,256]{1,0:T(8,128)S(1)} collective-permute-done((f32[128,256]{1,0:T(8,128)S(1)}, f32[128,256]{1,0:T(8,128)S(1)}, u32[]{:S(2)}, u32[]{:S(2)}) %collective-permute-start.32) | collective-permute-done | bytes 131104 | tf_op jit(solution)/shard_map/ppermute | solution.py:20
  135.1 2.7 %shard_map.91 = f32[256,1024]{1,0:T(8,128)} custom-call(f32[2,512,256]{2,1,0:T(8,128)S(1)} %copy-done.1, f32[128,256]{1,0:T(8,128)S(1)} %select_add_fusion.7.refs_0_, f32[128,256]{1,0:T(8,128)S(1)} %select_add_fusion.6.refs_1_, f32[128,256]{1,0:T(8,128)S(1)} %select_add_fusion.5.refs_2_, f32[128,256]{1,0:T(8,128)S(1)} %select_add_fusion.4.refs_3_), custom_call_target="tpu_custom_call" | custom-call | tf_op jit(solution)/shard_map/pallas_call | solution.py:152
  (96 shorter events, 35.6 us)
Async XLA Ops:
  2.0 14.9 %collective-permute-start = (f32[512,256]{1,0:T(8,128)S(1)}, f32[512,256]{1,0:T(8,128)S(1)}, u32[]{:S(2)}, u32[]{:S(2)}) collective-permute-start(f32[512,256]{1,0:T(8,128)S(1)} %shard_map.65), channel_id=1, source_target_pairs={{0,64},{64,0},{128,192},{192,128},{1,65},{65,1},{129,193},{193,129... | collective-permute-start | bytes 1572872 | tf_op jit(solution)/shard_map/ppermute | solution.py:20
  5.6 22.5 %collective-permute-start.2 = (f32[512,256]{1,0:T(8,128)S(1)}, f32[512,256]{1,0:T(8,128)S(1)}, u32[]{:S(2)}, u32[]{:S(2)}) collective-permute-start(f32[512,256]{1,0:T(8,128)S(1)} %shard_map.66), channel_id=1, source_target_pairs={{0,64},{64,0},{128,192},{192,128},{1,65},{65,1},{129,193},{193,129... | collective-permute-start | bytes 1572872 | tf_op jit(solution)/shard_map/ppermute | solution.py:20
  8.3 31.1 %collective-permute-start.5 = (f32[512,256]{1,0:T(8,128)S(1)}, f32[512,256]{1,0:T(8,128)S(1)}, u32[]{:S(2)}, u32[]{:S(2)}) collective-permute-start(f32[512,256]{1,0:T(8,128)S(1)} %shard_map.67), channel_id=1, source_target_pairs={{0,64},{64,0},{128,192},{192,128},{1,65},{65,1},{129,193},{193,129... | collective-permute-start | bytes 1572872 | tf_op jit(solution)/shard_map/ppermute | solution.py:20
  11.9 37.6 %collective-permute-start.9 = (f32[512,256]{1,0:T(8,128)S(1)}, f32[512,256]{1,0:T(8,128)S(1)}, u32[]{:S(2)}, u32[]{:S(2)}) collective-permute-start(f32[512,256]{1,0:T(8,128)S(1)} %shard_map.68), channel_id=1, source_target_pairs={{0,64},{64,0},{128,192},{192,128},{1,65},{65,1},{129,193},{193,129... | collective-permute-start | bytes 1572872 | tf_op jit(solution)/shard_map/ppermute | solution.py:20
  17.0 14.1 %collective-permute-start.1 = (f32[512,256]{1,0:T(8,128)S(1)}, f32[512,256]{1,0:T(8,128)S(1)}, u32[]{:S(2)}, u32[]{:S(2)}) collective-permute-start(f32[512,256]{1,0:T(8,128)S(1)} %broadcast_select_fusion.3), channel_id=1, source_target_pairs={{0,192},{64,128},{128,64},{192,0},{1,193},{65,129},{129,65},{193,1... | collective-permute-start | bytes 1572872 | tf_op jit(solution)/shard_map/ppermute | solution.py:20
  19.9 35.2 %collective-permute-start.10 = (f32[2,256,512]{2,1,0:T(8,128)S(1)}, f32[2,256,512]{2,1,0:T(8,128)S(1)}, u32[]{:S(2)}, u32[]{:S(2)}) collective-permute-start(f32[2,256,512]{2,1,0:T(8,128)S(1)} %slice_bitcast_fusion), channel_id=1, source_target_pairs={{0,2},{1,3},{2,0},{3,1},{4,6},{5,7},{6,4},{7,5},{8,10},{9,11},{10,... | collective-permute-start | bytes 3145736 | tf_op jit(solution)/shard_map/ppermute | solution.py:20
  28.2 14.1 %collective-permute-start.4 = (f32[512,256]{1,0:T(8,128)S(1)}, f32[512,256]{1,0:T(8,128)S(1)}, u32[]{:S(2)}, u32[]{:S(2)}) collective-permute-start(f32[512,256]{1,0:T(8,128)S(1)} %broadcast_select_fusion.2), channel_id=1, source_target_pairs={{0,192},{64,128},{128,64},{192,0},{1,193},{65,129},{129,65},{193,1... | collective-permute-start | bytes 1572872 | tf_op jit(solution)/shard_map/ppermute | solution.py:20
  31.2 11.3 %collective-permute-start.3 = (f32[512,256]{1,0:T(8,128)S(1)}, f32[512,256]{1,0:T(8,128)S(1)}, u32[]{:S(2)}, u32[]{:S(2)}) collective-permute-start(f32[512,256]{1,0:T(8,128)S(1)} %select_select_fusion.3.a), channel_id=1, source_target_pairs={{0,1},{1,0},{2,3},{3,2},{4,5},{5,4},{6,7},{7,6},{8,9},{9,8},{10,11... | collective-permute-start | bytes 1572872 | tf_op jit(solution)/shard_map/ppermute | solution.py:20
  39.5 12.9 %collective-permute-start.8 = (f32[512,256]{1,0:T(8,128)S(1)}, f32[512,256]{1,0:T(8,128)S(1)}, u32[]{:S(2)}, u32[]{:S(2)}) collective-permute-start(f32[512,256]{1,0:T(8,128)S(1)} %broadcast_select_fusion.1), channel_id=1, source_target_pairs={{0,192},{64,128},{128,64},{192,0},{1,193},{65,129},{129,65},{193,1... | collective-permute-start | bytes 1572872 | tf_op jit(solution)/shard_map/ppermute | solution.py:20
  42.4 10.2 %collective-permute-start.7 = (f32[512,256]{1,0:T(8,128)S(1)}, f32[512,256]{1,0:T(8,128)S(1)}, u32[]{:S(2)}, u32[]{:S(2)}) collective-permute-start(f32[512,256]{1,0:T(8,128)S(1)} %select_select_fusion.2.a), channel_id=1, source_target_pairs={{0,1},{1,0},{2,3},{3,2},{4,5},{5,4},{6,7},{7,6},{8,9},{9,8},{10,11... | collective-permute-start | bytes 1572872 | tf_op jit(solution)/shard_map/ppermute | solution.py:20
  43.2 14.8 %collective-permute-start.6 = (f32[512,256]{1,0:T(8,128)S(1)}, f32[512,256]{1,0:T(8,128)S(1)}, u32[]{:S(2)}, u32[]{:S(2)}) collective-permute-start(f32[512,256]{1,0:T(8,128)S(1)} %shard_map.70.a.b), channel_id=1, source_target_pairs={{0,2},{1,3},{2,0},{3,1},{4,6},{5,7},{6,4},{7,5},{8,10},{9,11},{10,... | collective-permute-start | bytes 1572872 | tf_op jit(solution)/shard_map/ppermute | solution.py:20
  49.5 14.1 %collective-permute-start.14 = (f32[512,256]{1,0:T(8,128)S(1)}, f32[512,256]{1,0:T(8,128)S(1)}, u32[]{:S(2)}, u32[]{:S(2)}) collective-permute-start(f32[512,256]{1,0:T(8,128)S(1)} %broadcast_select_fusion), channel_id=1, source_target_pairs={{0,192},{64,128},{128,64},{192,0},{1,193},{65,129},{129,65},{193,1... | collective-permute-start | bytes 1572872 | tf_op jit(solution)/shard_map/ppermute | solution.py:20
  52.5 11.3 %collective-permute-start.13 = (f32[512,256]{1,0:T(8,128)S(1)}, f32[512,256]{1,0:T(8,128)S(1)}, u32[]{:S(2)}, u32[]{:S(2)}) collective-permute-start(f32[512,256]{1,0:T(8,128)S(1)} %select_select_fusion.1.a), channel_id=1, source_target_pairs={{0,1},{1,0},{2,3},{3,2},{4,5},{5,4},{6,7},{7,6},{8,9},{9,8},{10,11... | collective-permute-start | bytes 1572872 | tf_op jit(solution)/shard_map/ppermute | solution.py:20
  53.3 15.9 %collective-permute-start.12 = (f32[512,256]{1,0:T(8,128)S(1)}, f32[512,256]{1,0:T(8,128)S(1)}, u32[]{:S(2)}, u32[]{:S(2)}) collective-permute-start(f32[512,256]{1,0:T(8,128)S(1)} %shard_map.71.b.a), channel_id=1, source_target_pairs={{0,2},{1,3},{2,0},{3,1},{4,6},{5,7},{6,4},{7,5},{8,10},{9,11},{10,... | collective-permute-start | bytes 1572872 | tf_op jit(solution)/shard_map/ppermute | solution.py:20
  58.6 15.0 %collective-permute-start.11 = (f32[512,256]{1,0:T(8,128)S(1)}, f32[512,256]{1,0:T(8,128)S(1)}, u32[]{:S(2)}, u32[]{:S(2)}) collective-permute-start(f32[512,256]{1,0:T(8,128)S(1)} %shard_map.74), channel_id=1, source_target_pairs={{0,6},{1,7},{2,4},{3,5},{4,2},{5,3},{6,0},{7,1},{8,14},{9,15},{10,... | collective-permute-start | bytes 1572872 | tf_op jit(solution)/shard_map/ppermute | solution.py:20
  63.8 13.1 %collective-permute-start.18 = (f32[512,256]{1,0:T(8,128)S(1)}, f32[512,256]{1,0:T(8,128)S(1)}, u32[]{:S(2)}, u32[]{:S(2)}) collective-permute-start(f32[512,256]{1,0:T(8,128)S(1)} %select_select_fusion.a), channel_id=1, source_target_pairs={{0,1},{1,0},{2,3},{3,2},{4,5},{5,4},{6,7},{7,6},{8,9},{9,8},{10,11... | collective-permute-start | bytes 1572872 | tf_op jit(solution)/shard_map/ppermute | solution.py:20
  64.5 16.0 %collective-permute-start.17 = (f32[512,256]{1,0:T(8,128)S(1)}, f32[512,256]{1,0:T(8,128)S(1)}, u32[]{:S(2)}, u32[]{:S(2)}) collective-permute-start(f32[512,256]{1,0:T(8,128)S(1)} %shard_map.75.b.a), channel_id=1, source_target_pairs={{0,2},{1,3},{2,0},{3,1},{4,6},{5,7},{6,4},{7,5},{8,10},{9,11},{10,... | collective-permute-start | bytes 1572872 | tf_op jit(solution)/shard_map/ppermute | solution.py:20
  69.8 14.5 %collective-permute-start.16 = (f32[512,256]{1,0:T(8,128)S(1)}, f32[512,256]{1,0:T(8,128)S(1)}, u32[]{:S(2)}, u32[]{:S(2)}) collective-permute-start(f32[512,256]{1,0:T(8,128)S(1)} %shard_map.76), channel_id=1, source_target_pairs={{0,6},{1,7},{2,4},{3,5},{4,2},{5,3},{6,0},{7,1},{8,14},{9,15},{10,... | collective-permute-start | bytes 1572872 | tf_op jit(solution)/shard_map/ppermute | solution.py:20
  74.2 13.7 %collective-permute-start.15 = (f32[512,256]{1,0:T(8,128)S(1)}, f32[512,256]{1,0:T(8,128)S(1)}, u32[]{:S(2)}, u32[]{:S(2)}) collective-permute-start(f32[512,256]{1,0:T(8,128)S(1)} %shard_map.77.a), channel_id=1, source_target_pairs={{0,8},{1,9},{2,10},{3,11},{4,12},{5,13},{6,14},{7,15},{8,0},{9,1},... | collective-permute-start | bytes 1572872 | tf_op jit(solution)/shard_map/ppermute | solution.py:20
  77.5 13.8 %collective-permute-start.22 = (f32[512,256]{1,0:T(8,128)S(1)}, f32[512,256]{1,0:T(8,128)S(1)}, u32[]{:S(2)}, u32[]{:S(2)}) collective-permute-start(f32[512,256]{1,0:T(8,128)S(1)} %shard_map.79.b.a), channel_id=1, source_target_pairs={{0,2},{1,3},{2,0},{3,1},{4,6},{5,7},{6,4},{7,5},{8,10},{9,11},{10,... | collective-permute-start | bytes 1572872 | tf_op jit(solution)/shard_map/ppermute | solution.py:20
  81.1 14.6 %collective-permute-start.21 = (f32[512,256]{1,0:T(8,128)S(1)}, f32[512,256]{1,0:T(8,128)S(1)}, u32[]{:S(2)}, u32[]{:S(2)}) collective-permute-start(f32[512,256]{1,0:T(8,128)S(1)} %shard_map.80), channel_id=1, source_target_pairs={{0,6},{1,7},{2,4},{3,5},{4,2},{5,3},{6,0},{7,1},{8,14},{9,15},{10,... | collective-permute-start | bytes 1572872 | tf_op jit(solution)/shard_map/ppermute | solution.py:20
  85.0 13.9 %collective-permute-start.20 = (f32[512,256]{1,0:T(8,128)S(1)}, f32[512,256]{1,0:T(8,128)S(1)}, u32[]{:S(2)}, u32[]{:S(2)}) collective-permute-start(f32[512,256]{1,0:T(8,128)S(1)} %shard_map.81.a), channel_id=1, source_target_pairs={{0,8},{1,9},{2,10},{3,11},{4,12},{5,13},{6,14},{7,15},{8,0},{9,1},... | collective-permute-start | bytes 1572872 | tf_op jit(solution)/shard_map/ppermute | solution.py:20
  88.5 12.0 %collective-permute-start.19 = (f32[256,256]{1,0:T(8,128)S(1)}, f32[256,256]{1,0:T(8,128)S(1)}, u32[]{:S(2)}, u32[]{:S(2)}) collective-permute-start(f32[256,256]{1,0:T(8,128)S(1)} %slice_select_fusion.3), channel_id=1, source_target_pairs={{0,64},{64,0},{128,192},{192,128},{1,65},{65,1},{129,193},{193,129... | collective-permute-start | bytes 786440 | tf_op jit(solution)/shard_map/ppermute | solution.py:20
  91.9 14.9 %collective-permute-start.26 = (f32[512,256]{1,0:T(8,128)S(1)}, f32[512,256]{1,0:T(8,128)S(1)}, u32[]{:S(2)}, u32[]{:S(2)}) collective-permute-start(f32[512,256]{1,0:T(8,128)S(1)} %shard_map.84), channel_id=1, source_target_pairs={{0,6},{1,7},{2,4},{3,5},{4,2},{5,3},{6,0},{7,1},{8,14},{9,15},{10,... | collective-permute-start | bytes 1572872 | tf_op jit(solution)/shard_map/ppermute | solution.py:20
  96.3 14.0 %collective-permute-start.25 = (f32[512,256]{1,0:T(8,128)S(1)}, f32[512,256]{1,0:T(8,128)S(1)}, u32[]{:S(2)}, u32[]{:S(2)}) collective-permute-start(f32[512,256]{1,0:T(8,128)S(1)} %shard_map.85.a), channel_id=1, source_target_pairs={{0,8},{1,9},{2,10},{3,11},{4,12},{5,13},{6,14},{7,15},{8,0},{9,1},... | collective-permute-start | bytes 1572872 | tf_op jit(solution)/shard_map/ppermute | solution.py:20
  100.2 11.1 %collective-permute-start.24 = (f32[256,256]{1,0:T(8,128)S(1)}, f32[256,256]{1,0:T(8,128)S(1)}, u32[]{:S(2)}, u32[]{:S(2)}) collective-permute-start(f32[256,256]{1,0:T(8,128)S(1)} %slice_select_fusion.2), channel_id=1, source_target_pairs={{0,64},{64,0},{128,192},{192,128},{1,65},{65,1},{129,193},{193,129... | collective-permute-start | bytes 786440 | tf_op jit(solution)/shard_map/ppermute | solution.py:20
  100.6 12.2 %collective-permute-start.23 = (f32[128,256]{1,0:T(8,128)S(1)}, f32[128,256]{1,0:T(8,128)S(1)}, u32[]{:S(2)}, u32[]{:S(2)}) collective-permute-start(f32[128,256]{1,0:T(8,128)S(1)} %slice_select_fusion.7), channel_id=1, source_target_pairs={{0,192},{64,128},{128,64},{192,0},{1,193},{65,129},{129,65},{193,1... | collective-permute-start | bytes 393224 | tf_op jit(solution)/shard_map/ppermute | solution.py:20
  107.4 13.6 %collective-permute-start.29 = (f32[512,256]{1,0:T(8,128)S(1)}, f32[512,256]{1,0:T(8,128)S(1)}, u32[]{:S(2)}, u32[]{:S(2)}) collective-permute-start(f32[512,256]{1,0:T(8,128)S(1)} %shard_map.88.a), channel_id=1, source_target_pairs={{0,8},{1,9},{2,10},{3,11},{4,12},{5,13},{6,14},{7,15},{8,0},{9,1},... | collective-permute-start | bytes 1572872 | tf_op jit(solution)/shard_map/ppermute | solution.py:20
  111.0 11.0 %collective-permute-start.28 = (f32[256,256]{1,0:T(8,128)S(1)}, f32[256,256]{1,0:T(8,128)S(1)}, u32[]{:S(2)}, u32[]{:S(2)}) collective-permute-start(f32[256,256]{1,0:T(8,128)S(1)} %slice_select_fusion.1), channel_id=1, source_target_pairs={{0,64},{64,0},{128,192},{192,128},{1,65},{65,1},{129,193},{193,129... | collective-permute-start | bytes 786440 | tf_op jit(solution)/shard_map/ppermute | solution.py:20
  111.4 12.4 %collective-permute-start.27 = (f32[128,256]{1,0:T(8,128)S(1)}, f32[128,256]{1,0:T(8,128)S(1)}, u32[]{:S(2)}, u32[]{:S(2)}) collective-permute-start(f32[128,256]{1,0:T(8,128)S(1)} %slice_select_fusion.6), channel_id=1, source_target_pairs={{0,192},{64,128},{128,64},{192,0},{1,193},{65,129},{129,65},{193,1... | collective-permute-start | bytes 393224 | tf_op jit(solution)/shard_map/ppermute | solution.py:20
  121.7 7.0 %collective-permute-start.31 = (f32[256,256]{1,0:T(8,128)S(1)}, f32[256,256]{1,0:T(8,128)S(1)}, u32[]{:S(2)}, u32[]{:S(2)}) collective-permute-start(f32[256,256]{1,0:T(8,128)S(1)} %slice_select_fusion), channel_id=1, source_target_pairs={{0,64},{64,0},{128,192},{192,128},{1,65},{65,1},{129,193},{193,129... | collective-permute-start | bytes 786440 | tf_op jit(solution)/shard_map/ppermute | solution.py:20
  122.1 8.5 %collective-permute-start.30 = (f32[128,256]{1,0:T(8,128)S(1)}, f32[128,256]{1,0:T(8,128)S(1)}, u32[]{:S(2)}, u32[]{:S(2)}) collective-permute-start(f32[128,256]{1,0:T(8,128)S(1)} %slice_select_fusion.5), channel_id=1, source_target_pairs={{0,192},{64,128},{128,64},{192,0},{1,193},{65,129},{129,65},{193,1... | collective-permute-start | bytes 393224 | tf_op jit(solution)/shard_map/ppermute | solution.py:20
  (5 other events, 58.0 us)
